TPU v7x, 256 devices: a whole 4x4x8 slice. The times are simulated.
256 devices in a mesh: dp: 32 (over z_hi, y, core), expert: 8 (over x, z_lo).
Axes of the slice: x: 4, y: 4, z: 8 (z_hi: 4, z_lo: 2; z = z_hi * 2 + z_lo), core: 2. Of those that a mesh axis runs over, the one named last changes fastest.
Arguments:
- tokens: bfloat16 [49152, 2048], P(('dp', 'expert')), may hold values from -24 to 24
- routes: int32 [49152, 6], P(('dp', 'expert')), may hold values from 0 to 63, as said below
- gate_scale: float32 [49152, 6], P(('dp', 'expert')), may hold values from 0.2 to 2
- w_gate: bfloat16 [8, 2048, 768], P('expert', 'dp'), may hold values from -0.125 to 0.125
- w_up: bfloat16 [8, 2048, 768], P('expert', 'dp'), may hold values from -0.125 to 0.125
- w_down: bfloat16 [8, 2048, 768], P('expert', 'dp'), may hold values from -0.21875 to 0.21875
- d_out: bfloat16 [49152, 2048], P(('dp', 'expert')), may hold values from -24 to 24
Outputs:
- layer_out: bfloat16 [49152, 2048], P(('dp', 'expert'))
- d_tokens: bfloat16 [49152, 2048], P(('dp', 'expert'))
- grad_gate: float32 [8, 2048, 768], P('expert', 'dp')
- grad_up: float32 [8, 2048, 768], P('expert', 'dp')
- grad_down: float32 [8, 2048, 768], P('expert', 'dp')
Inputs may be any that keep to these rules, and one draw needn't show every extreme that they name: `routes`: each token names 6 different experts. The experts of this window are 0 to 7; among the 192 tokens of one device no window expert is named by more than 32 tokens.
All inputs are finite; a program needn't handle non-finite values.
Results may differ from a plain program's by a relative error of at most 0.02.
Values may be sent and summed in bfloat16 or wider, within the bound.
A program may use at most 64 MiB of HBM per device.

v0:
```python
import jax
import jax.numpy as jnp
from jax import lax
from jax.sharding import PartitionSpec as P

CAP = 32


def shards(tokens, routes, gate_scale, w_gate, w_up, w_down, d_out):
    experts_here = lax.axis_size("expert")
    tok_count = tokens.shape[0]
    width = tokens.shape[1]
    choices_per = routes.shape[1]
    capacity = CAP
    slots = experts_here * capacity
    flat_count = tok_count * choices_per
    combine = gate_scale / jnp.sum(gate_scale, axis=1, keepdims=True)
    flat_ids = routes.reshape(flat_count)
    flat_weight = combine.reshape(flat_count)
    live = flat_ids < experts_here
    onehot = (
        (flat_ids[:, None] == jnp.arange(experts_here, dtype=jnp.int32)[None, :]) & live[:, None]
    ).astype(jnp.int32)
    position = jnp.sum((jnp.cumsum(onehot, axis=0) - onehot) * onehot, axis=1)
    dest = jnp.where(live, flat_ids * capacity + position, slots)
    match = jnp.arange(slots, dtype=jnp.int32)[:, None] == dest[None, :]
    filled = jnp.any(match, axis=1)
    owner = jnp.sum(
        jnp.where(match, (jnp.arange(flat_count, dtype=jnp.int32) // choices_per)[None, :], 0),
        axis=1,
    )
    slot_weight = jnp.sum(jnp.where(match, flat_weight[None, :], 0.0), axis=1)
    send_x = jnp.where(filled[:, None], tokens[owner], jnp.zeros((), jnp.bfloat16))
    send_d = jnp.where(
        filled[:, None], d_out[owner].astype(jnp.float32) * slot_weight[:, None], 0.0
    ).astype(jnp.bfloat16)
    send_x = send_x.reshape(experts_here, capacity, width)
    send_d = send_d.reshape(experts_here, capacity, width)
    full_gate, full_up, full_down = (
        lax.all_gather(w_gate, "dp", axis=1, tiled=True),
        lax.all_gather(w_up, "dp", axis=1, tiled=True),
        lax.all_gather(w_down, "dp", axis=1, tiled=True),
    )
    recv_x, recv_d = (
        lax.all_to_all(send_x, "expert", split_axis=0, concat_axis=0, tiled=True),
        lax.all_to_all(send_d, "expert", split_axis=0, concat_axis=0, tiled=True),
    )
    weight_gate = full_gate[0]
    weight_up = full_up[0]
    weight_down = full_down[0]
    rows_x = recv_x.reshape(slots, width)
    rows_d = recv_d.reshape(slots, width)
    contract_last = (((1,), (1,)), ((), ()))
    contract_first = (((0,), (0,)), ((), ()))
    gate = jnp.dot(rows_x, weight_gate, preferred_element_type=jnp.float32)
    up = jnp.dot(rows_x, weight_up, preferred_element_type=jnp.float32)
    sig = jax.nn.sigmoid(gate)
    act = gate * sig
    hidden = (act * up).astype(jnp.bfloat16)
    expert_out = lax.dot_general(
        hidden, weight_down, contract_last, preferred_element_type=jnp.float32
    ).astype(jnp.bfloat16)
    d_hidden = jnp.dot(rows_d, weight_down, preferred_element_type=jnp.float32)
    d_gate = (d_hidden * up * sig * (1.0 + gate * (1.0 - sig))).astype(jnp.bfloat16)
    d_up = (d_hidden * act).astype(jnp.bfloat16)
    d_in = (
        lax.dot_general(d_gate, weight_gate, contract_last, preferred_element_type=jnp.float32)
        + lax.dot_general(d_up, weight_up, contract_last, preferred_element_type=jnp.float32)
    ).astype(jnp.bfloat16)
    back_out, back_in = (
        lax.all_to_all(
            expert_out.reshape(experts_here, capacity, width),
            "expert",
            split_axis=0,
            concat_axis=0,
            tiled=True,
        ),
        lax.all_to_all(
            d_in.reshape(experts_here, capacity, width),
            "expert",
            split_axis=0,
            concat_axis=0,
            tiled=True,
        ),
    )
    term_gate = lax.dot_general(rows_x, d_gate, contract_first, preferred_element_type=jnp.float32)
    term_up = lax.dot_general(rows_x, d_up, contract_first, preferred_element_type=jnp.float32)
    term_down = lax.dot_general(rows_d, hidden, contract_first, preferred_element_type=jnp.float32)
    grad_gate, grad_up, grad_down = (
        lax.psum_scatter(
            term_gate.astype(jnp.bfloat16), "dp", scatter_dimension=0, tiled=True
        ).astype(jnp.float32),
        lax.psum_scatter(
            term_up.astype(jnp.bfloat16), "dp", scatter_dimension=0, tiled=True
        ).astype(jnp.float32),
        lax.psum_scatter(
            term_down.astype(jnp.bfloat16), "dp", scatter_dimension=0, tiled=True
        ).astype(jnp.float32),
    )
    back_out = back_out.reshape(slots, width)
    back_in = back_in.reshape(slots, width)
    dest_tok = dest.reshape(tok_count, choices_per)
    live_tok = live.reshape(tok_count, choices_per)
    weight_tok = jnp.where(live_tok, combine, 0.0)
    safe_rows = jnp.where(live_tok, dest_tok, 0)
    total_out = jnp.zeros((tok_count, width), jnp.float32)
    total_in = jnp.zeros((tok_count, width), jnp.float32)
    for choice_index in range(choices_per):
        rows_pick = safe_rows[:, choice_index]
        total_out = total_out + weight_tok[:, choice_index : choice_index + 1] * back_out[
            rows_pick
        ].astype(jnp.float32)
        total_in = total_in + jnp.where(
            live_tok[:, choice_index : choice_index + 1],
            back_in[rows_pick].astype(jnp.float32),
            0.0,
        )
    layer_out = total_out.astype(jnp.bfloat16)
    d_tokens = total_in.astype(jnp.bfloat16)
    return (layer_out, d_tokens, grad_gate[None], grad_up[None], grad_down[None])


def solution(mesh):
    placed = (
        P(("dp", "expert"), None),
        P(("dp", "expert"), None),
        P(("dp", "expert"), None),
        P("expert", "dp", None),
        P("expert", "dp", None),
        P("expert", "dp", None),
        P(("dp", "expert"), None),
    )
    return jax.shard_map(
        shards,
        mesh=mesh,
        in_specs=placed,
        out_specs=(
            P(("dp", "expert"), None),
            P(("dp", "expert"), None),
            P("expert", "dp", None),
            P("expert", "dp", None),
            P("expert", "dp", None),
        ),
        check_vma=False,
    )
```

profile of v0, /device:TPU:1, one launch (start us, length us, event | category | flops | bytes accessed | tf_op | source)
XLA Modules:
  0.0 493.0 jit_solution(7565816909941220168)
XLA Ops:
  9.4 0.8 copy.30
  10.5 2.3 reduce-window.6
  16.0 1.4 gather_fusion.7
  17.3 1.3 fusion.22
  18.6 6.3 %all-to-all-start.2 = ((bf16[8,32,2048]{2,1,0:T(8,128)(2,1)}), bf16[8,32,2048]{2,1,0:T(8,128)(2,1)S(1)}, u32[]{:S(2)}, u32[]{:S(2)}) async-start(bf16[8,32,2048]{2,1,0:T(8,128)(2,1)} %fusion.22), calls=%async_computation.2 | async-start | bytes 2097152 | tf_op jit(solution)/shard_map/all_to_all | solution.py:46
  25.0 2.3 gather_fusion
  27.3 2.4 broadcast_select_fusion
  29.7 12.8 %all-to-all-done.2 = bf16[8,32,2048]{2,1,0:T(8,128)(2,1)S(1)} async-done(((bf16[8,32,2048]{2,1,0:T(8,128)(2,1)}), bf16[8,32,2048]{2,1,0:T(8,128)(2,1)S(1)}, u32[]{:S(2)}, u32[]{:S(2)}) %all-to-all-start.2) | async-done | bytes 1048608 | tf_op jit(solution)/shard_map/all_to_all | solution.py:46
  42.5 1.0 copy-done.2
  43.5 3.6 all-to-all-start
  47.1 29.7 %all-gather.8.cloned.1.call-done = bf16[1,2048,768]{2,1,0:T(8,128)(2,1)} async-done(((bf16[1,64,768]{2,1,0:T(8,128)(2,1)}), bf16[1,2048,768]{2,1,0:T(8,128)(2,1)}) %all-gather.8.cloned.1.call-update) | async-done | bytes 3145744 | tf_op jit(solution)/shard_map/all_gather | solution.py:42
  76.8 4.1 fusion
  80.8 52.9 %all-gather.6.cloned.1.call-done = bf16[1,2048,768]{2,1,0:T(8,128)(2,1)} async-done(((bf16[1,64,768]{2,1,0:T(8,128)(2,1)}), bf16[1,2048,768]{2,1,0:T(8,128)(2,1)}) %all-gather.6.cloned.1.call-update) | async-done | bytes 3145744 | tf_op jit(solution)/shard_map/all_gather | solution.py:41
  133.8 3.7 fusion.6
  137.5 53.7 %all-gather.4.cloned.1.call-done = bf16[1,2048,768]{2,1,0:T(8,128)(2,1)} async-done(((bf16[1,64,768]{2,1,0:T(8,128)(2,1)}), bf16[1,2048,768]{2,1,0:T(8,128)(2,1)}) %all-gather.4.cloned.1.call-update) | async-done | bytes 3145744 | tf_op jit(solution)/shard_map/all_gather | solution.py:40
  191.2 4.3 multiply_convert_fusion.1
  196.2 2.8 convolution_convert_fusion
  199.0 2.7 convolution_convert_fusion.2
  201.8 1.0 copy-done.12
  202.7 3.0 fusion.4
  205.8 2.1 fusion.15
  207.9 4.5 all-to-all-start.3
  212.6 2.7 convolution_convert_fusion.1
  215.4 1.0 copy-done.15
  216.4 3.9 fusion.18
  220.3 7.4 %all-to-all-done.3 = bf16[8,32,2048]{2,1,0:T(8,128)(2,1)S(1)} async-done(((bf16[8,32,2048]{2,1,0:T(8,128)(2,1)}), bf16[8,32,2048]{2,1,0:T(8,128)(2,1)S(1)}, u32[]{:S(2)}, u32[]{:S(2)}) %all-to-all-start.3) | async-done | bytes 1048608 | tf_op jit(solution)/shard_map/all_to_all | solution.py:78
  227.7 3.6 all-to-all-start.1
  231.7 2.0 gather_fusion.13
  233.7 11.6 %all-to-all-done.1 = bf16[8,32,2048]{2,1,0:T(8,128)(2,1)S(1)} async-done(((bf16[8,32,2048]{2,1,0:T(8,128)(2,1)}), bf16[8,32,2048]{2,1,0:T(8,128)(2,1)S(1)}, u32[]{:S(2)}, u32[]{:S(2)}) %all-to-all-start.1) | async-done | bytes 1048608 | tf_op jit(solution)/shard_map/all_to_all | solution.py:71
  245.3 2.0 gather_fusion.6
  247.3 2.0 gather_fusion.12
  249.3 2.0 gather_fusion.5
  251.4 2.0 gather_fusion.11
  253.4 2.1 gather_fusion.4
  255.4 2.0 gather_fusion.10
  257.5 2.0 gather_fusion.3
  259.5 2.1 gather_fusion.8
  261.6 2.0 gather_fusion.1
  263.6 2.1 gather_fusion.9
  265.7 2.1 gather_fusion.2
  267.8 4.1 add_convert_fusion
  271.9 1.9 add_convert_fusion.1
  273.8 16.4 %reduce-scatter.8.cloned.1.call-done = bf16[64,768]{1,0:T(8,128)(2,1)} async-done(((bf16[2048,768]{1,0:T(8,128)(2,1)}), bf16[64,768]{1,0:T(8,128)(2,1)}) %reduce-scatter.8.cloned.1.call-update) | async-done | bytes 98320 | tf_op jit(solution)/shard_map/reduce_scatter | solution.py:96
  290.2 1.6 bitcast_convert_fusion
  291.8 95.8 %reduce-scatter.4.cloned.1.call-done = bf16[64,768]{1,0:T(8,128)(2,1)} async-done(((bf16[2048,768]{1,0:T(8,128)(2,1)}), bf16[64,768]{1,0:T(8,128)(2,1)}) %reduce-scatter.4.cloned.1.call-update) | async-done | bytes 98320 | tf_op jit(solution)/shard_map/reduce_scatter | solution.py:90
  387.6 1.6 bitcast_convert_fusion.2
  389.2 95.3 %reduce-scatter.6.cloned.1.call-done = bf16[64,768]{1,0:T(8,128)(2,1)} async-done(((bf16[2048,768]{1,0:T(8,128)(2,1)}), bf16[64,768]{1,0:T(8,128)(2,1)}) %reduce-scatter.6.cloned.1.call-update) | async-done | bytes 98320 | tf_op jit(solution)/shard_map/reduce_scatter | solution.py:93
  484.5 1.6 bitcast_convert_fusion.1
  (77 shorter events, 7.0 us)
Async XLA Ops:
  7.2 8.8 %copy-start = (bf16[192,2048]{1,0:T(8,128)(2,1)S(1)}, bf16[192,2048]{1,0:T(8,128)(2,1)}, u32[]{:S(2)}) copy-start(bf16[192,2048]{1,0:T(8,128)(2,1)} %param.13) | copy-start | bytes 2359300
  7.2 69.6 %all-gather.8.cloned.1.call-start = ((), (), s32[]{:S(2)}) async-start(), calls=%async_computation.9 | async-start | bytes 3244032 | tf_op jit(solution)/shard_map/all_gather | solution.py:42
  7.9 125.9 %all-gather.6.cloned.1.call-start = ((), (), s32[]{:S(2)}) async-start(), calls=%async_computation.8 | async-start | bytes 3244032 | tf_op jit(solution)/shard_map/all_gather | solution.py:41
  8.7 182.5 %all-gather.4.cloned.1.call-start = ((), (), s32[]{:S(2)}) async-start(), calls=%async_computation.7 | async-start | bytes 3244032 | tf_op jit(solution)/shard_map/all_gather | solution.py:40
  18.6 6.3 %copy-start.1 = (bf16[192,2048]{1,0:T(8,128)(2,1)S(1)}, bf16[192,2048]{1,0:T(8,128)(2,1)}, u32[]{:S(2)}) copy-start(bf16[192,2048]{1,0:T(8,128)(2,1)} %param.7) | copy-start | bytes 2359300
  18.6 23.9 %all-to-all-start.2 = ((bf16[8,32,2048]{2,1,0:T(8,128)(2,1)}), bf16[8,32,2048]{2,1,0:T(8,128)(2,1)S(1)}, u32[]{:S(2)}, u32[]{:S(2)}) async-start(bf16[8,32,2048]{2,1,0:T(8,128)(2,1)} %fusion.22), calls=%async_computation.2 | async-start | bytes 2097152 | tf_op jit(solution)/shard_map/all_to_all | solution.py:46
  42.5 1.0 copy-start.2
  43.5 37.4 %all-to-all-start = ((bf16[8,32,2048]{2,1,0:T(8,128)(2,1)}), bf16[8,32,2048]{2,1,0:T(8,128)(2,1)S(1)}, u32[]{:S(2)}, u32[]{:S(2)}) async-start(bf16[8,32,2048]{2,1,0:T(8,128)(2,1)} %broadcast_select_fusion), calls=%async_computation | async-start | bytes 2097152 | tf_op jit(solution)/shard_map/all_to_all | solution.py:45
  47.1 243.2 %reduce-scatter.8.cloned.1.call-start = ((), (), s32[]{:S(2)}) async-start(), calls=%async_computation.12 | async-start | bytes 3244032 | tf_op jit(solution)/shard_map/reduce_scatter | solution.py:96
  137.5 58.7 %copy-start.3 = (bf16[8,32,2048]{2,1,0:T(8,128)(2,1)S(1)}, bf16[8,32,2048]{2,1,0:T(8,128)(2,1)}, u32[]{:S(2)}) copy-start(bf16[8,32,2048]{2,1,0:T(8,128)(2,1)} %copy-done.2) | copy-start | bytes 3145732
  195.5 0.7 copy-start.14
  199.0 188.6 %reduce-scatter.4.cloned.1.call-start = ((), (), s32[]{:S(2)}) async-start(), calls=%async_computation.10 | async-start | bytes 3244032 | tf_op jit(solution)/shard_map/reduce_scatter | solution.py:90
  201.7 1.0 copy-start.12
  202.7 3.1 copy-start.4
  207.9 4.7 copy-start.13
  207.9 19.8 %all-to-all-start.3 = ((bf16[8,32,2048]{2,1,0:T(8,128)(2,1)}), bf16[8,32,2048]{2,1,0:T(8,128)(2,1)S(1)}, u32[]{:S(2)}, u32[]{:S(2)}) async-start(bf16[8,32,2048]{2,1,0:T(8,128)(2,1)} %bitcast.104), calls=%async_computation.3 | async-start | bytes 2097152 | tf_op jit(solution)/shard_map/all_to_all | solution.py:78
  212.4 272.1 %reduce-scatter.6.cloned.1.call-start = ((), (), s32[]{:S(2)}) async-start(), calls=%async_computation.11 | async-start | bytes 3244032 | tf_op jit(solution)/shard_map/reduce_scatter | solution.py:93
  215.4 1.0 copy-start.15
  220.3 11.2 %copy-start.16 = (s32[192,6]{0,1:T(8,128)S(1)}, s32[192,6]{0,1:T(8,128)}, u32[]{:S(2)}) copy-start(s32[192,6]{0,1:T(8,128)} %param.8) | copy-start | bytes 13828
  227.7 17.6 %all-to-all-start.1 = ((bf16[8,32,2048]{2,1,0:T(8,128)(2,1)}), bf16[8,32,2048]{2,1,0:T(8,128)(2,1)S(1)}, u32[]{:S(2)}, u32[]{:S(2)}) async-start(bf16[8,32,2048]{2,1,0:T(8,128)(2,1)} %bitcast.107), calls=%async_computation.1 | async-start | bytes 2097152 | tf_op jit(solution)/shard_map/all_to_all | solution.py:71
  265.7 2.1 copy-start.9
  267.7 4.1 copy-start.5
  267.7 4.1 copy-start.6
  267.7 4.1 copy-start.7
  267.7 4.1 copy-start.8
  267.8 4.1 copy-start.10
  267.8 4.1 copy-start.11
Sparse Core Ops, SparseCore 0:
  10.6 66.1 all-gather.7
  79.3 54.4 all-gather.5
  136.3 54.8 all-gather.3
  199.1 91.0 reduce-scatter.7
  294.5 93.0 reduce-scatter.3
  391.4 93.1 reduce-scatter.5
where the time goes:
time: 495 us; the launch traced here: 493 us
  waiting for transfers between devices  378 us (76%)
  local copies, waits for them, and re-layouts  33.9 us (7%)
  matrix products  29.4 us (6%)
  other arithmetic  19.2 us (4%)
  starting transfers between devices  18.4 us (4%)
  between operations  14.4 us (3%)
    reduce_scatter x1, waiting for transfers between devices, shards(): lax.psum_scatter(term_gate.astype(jnp.bfloat16), 'dp', scatter_dimension=...  95.8 us
    reduce_scatter x1, waiting for transfers between devices, shards(): lax.psum_scatter(term_up.astype(jnp.bfloat16), 'dp', scatter_dimension=0,...  95.3 us
    all_gather x1, waiting for transfers between devices, shards(): lax.all_gather(w_gate, 'dp', axis=1, tiled=True)  53.7 us
    all_gather x1, waiting for transfers between devices, shards(): lax.all_gather(w_up, 'dp', axis=1, tiled=True)  52.9 us
    all_gather x1, waiting for transfers between devices, shards(): lax.all_gather(w_down, 'dp', axis=1, tiled=True)  29.7 us
    reduce_scatter x1, waiting for transfers between devices, shards(): lax.psum_scatter(term_down.astype(jnp.bfloat16), 'dp', scatter_dimension=...  16.4 us
    all_to_all x1, waiting for transfers between devices, shards(): lax.all_to_all(send_d, 'expert', split_axis=0, concat_axis=0, tiled=True)  12.8 us
    gather x6, local copies, waits for them, and re-layouts, shards(): back_out[rows_pick].astype(jnp.float32)  12.3 us
  transfers between devices with their start and end apart: 10, of which 9 were waited for; matrix products, arithmetic and copies ran while one was open for 14% of the time, Pallas kernels for 0%

commit v1 on v0

v1 whole, which is shorter than its diff:
```python
import jax
import jax.numpy as jnp
from jax import lax
from jax.experimental import pallas as pl
from jax.experimental.pallas import tpu as pltpu
from jax.sharding import PartitionSpec as P

CAP = 32
MESH = pl.DeviceIdType.MESH
F32 = jnp.float32
BF16 = jnp.bfloat16

NY, NZ, SH = 4, 4, 128
HH = 384
HC = 3 * HH
YB = NZ * SH
NE = 8
TOK = 192
ROWS = NE * CAP

S_SIB = 0
S_LOC = 3
S_AGZ = 6
S_AGY = 10
S_A2X = 26
S_A2D = 34
S_SX = 42
S_SO = 44
S_BO = 46
S_BI = 54
S_RY1 = 62
S_RY2 = 70
S_RZ1 = 78
S_RZ2 = 80
S_FIN = 82
S_ALL = 83


def kernel(
    tok_ref, rt_ref, gs_ref, wg_ref, wu_ref, wd_ref, do_ref,
    lo_ref, dt_ref, gg_ref, gu_ref, gd_ref,
    W, X, D, XT, DT, SX, SD, SEL, ACC, CAT, T, R1, R2, Z1, Z2, ZS, FS, FR,
    OS, OR, BS, BK, ss, rs,
):
    i = lax.axis_index("dp")
    j = lax.axis_index("expert")
    c = lax.rem(i, 2)
    o = 1 - c
    p = lax.div(i, 2)
    y = lax.rem(p, 4)
    z = lax.div(p, 4)
    yp, ym, y2 = lax.rem(y + 1, 4), lax.rem(y + 3, 4), lax.rem(y + 2, 4)
    zp, zm, z2 = lax.rem(z + 1, 4), lax.rem(z + 3, 4), lax.rem(z + 2, 4)

    def place(yy, zz, cc):
        return {"dp": (zz * 4 + yy) * 2 + cc}

    sib = place(y, z, o)
    to_yp, to_ym = place(yp, z, c), place(ym, z, c)
    to_zp, to_zm = place(y, zp, c), place(y, zm, c)

    def peer(k):
        return lax.rem(j + k, NE)

    def source(k):
        return lax.rem(j + NE - k, NE)

    sent = []

    def send(src, dst, k, to):
        copy = pltpu.make_async_remote_copy(
            src_ref=src, dst_ref=dst, send_sem=ss.at[k], recv_sem=rs.at[k],
            device_id=to, device_id_type=MESH,
        )
        copy.start()
        sent.append(copy)

    def arrived(ref, k, to=None):
        pltpu.make_async_remote_copy(
            src_ref=ref, dst_ref=ref, send_sem=ss.at[k], recv_sem=rs.at[k],
            device_id=sib if to is None else to, device_id_type=MESH,
        ).wait_recv()

    barrier = pltpu.get_barrier_semaphore()
    for to in (sib, to_yp, to_ym, to_zp, to_zm):
        pl.semaphore_signal(barrier, inc=1, device_id=to, device_id_type=MESH)
    for k in range(1, NE):
        pl.semaphore_signal(barrier, inc=1, device_id={"expert": peer(k)}, device_id_type=MESH)
    pl.semaphore_wait(barrier, 5 + NE - 1)

    mine = pl.ds(pl.multiple_of(c * 64, 64), 64)
    theirs = pl.ds(pl.multiple_of(o * 64, 64), 64)
    half_c = pl.ds(pl.multiple_of(c * HH, 128), HH)
    half_o = pl.ds(pl.multiple_of(o * HH, 128), HH)
    local = []
    for n, w_ref in enumerate((wg_ref, wu_ref, wd_ref)):
        cols = pl.ds(n * HH, HH)
        send(w_ref.at[0, :, half_o], W.at[y, z, mine, cols], S_SIB + n, sib)
        copy = pltpu.make_async_copy(
            w_ref.at[0, :, half_c], W.at[y, z, mine, cols], rs.at[S_LOC + n]
        )
        copy.start()
        local.append(copy)
    for copy in local:
        copy.wait()
    for n in range(3):
        arrived(W.at[y, z, theirs, pl.ds(n * HH, HH)], S_SIB + n)

    low, high = pl.ds(0, 64), pl.ds(64, 64)

    def along_y(step, zz):
        send(W.at[y, zz], W.at[y, zz], S_AGY + 4 * step, to_yp)
        send(W.at[y, zz], W.at[y, zz], S_AGY + 4 * step + 1, to_ym)

    def onward_y(step, zz):
        arrived(W.at[ym, zz], S_AGY + 4 * step)
        send(W.at[ym, zz, low], W.at[ym, zz, low], S_AGY + 4 * step + 2, to_yp)
        arrived(W.at[yp, zz], S_AGY + 4 * step + 1)
        send(W.at[yp, zz, high], W.at[yp, zz, high], S_AGY + 4 * step + 3, to_ym)

    send(W.at[y, z], W.at[y, z], S_AGZ, to_zp)
    send(W.at[y, z], W.at[y, z], S_AGZ + 1, to_zm)
    along_y(0, z)

    shape = (TOK, ROWS)
    lane = lax.broadcasted_iota(jnp.int32, shape, 1)
    lane_e = lax.div(lane, CAP)
    lane_s = lax.rem(lane, CAP).astype(F32)
    scale = gs_ref[...]
    combine = scale / jnp.sum(scale, axis=1, keepdims=True)
    routes = rt_ref[...]
    named = jnp.zeros(shape, F32)
    weight = jnp.zeros(shape, F32)
    for s in range(6):
        same = routes[:, s:s + 1] == lane_e
        named = jnp.where(same, 1.0, named)
        weight = jnp.where(same, combine[:, s:s + 1], weight)
    earlier = (
        lax.broadcasted_iota(jnp.int32, (TOK, TOK), 1)
        < lax.broadcasted_iota(jnp.int32, (TOK, TOK), 0)
    ).astype(F32).astype(BF16)
    position = jnp.dot(earlier, named.astype(BF16), preferred_element_type=F32)
    chosen = jnp.where(position == lane_s, named, 0.0)
    weight = weight * chosen
    SEL[0] = chosen.astype(BF16)
    rest = weight
    for n in range(1, 4):
        part = rest.astype(BF16)
        SEL[n] = part
        rest = rest - part.astype(F32)

    tn = (((0,), (0,)), ((), ()))
    ones = jnp.ones((TOK, 128), BF16)
    slot_weight = sum(
        lax.dot_general(SEL[n], ones, tn, preferred_element_type=F32) for n in (3, 2, 1)
    )
    slot_weight = jnp.concatenate([slot_weight] * 4, axis=1)

    def columns(ref, yy):
        return jnp.concatenate(
            [ref[:, (zz * 4 + yy) * SH:(zz * 4 + yy + 1) * SH] for zz in range(NZ)], axis=1
        )

    for yy in range(NY):
        rows = lax.dot_general(SEL[0], columns(tok_ref, yy), tn, preferred_element_type=F32)
        SX[yy] = rows.astype(BF16).reshape(NE, CAP, YB)
        rows = lax.dot_general(SEL[0], columns(do_ref, yy), tn, preferred_element_type=F32)
        SD[yy] = (rows * slot_weight).astype(BF16).reshape(NE, CAP, YB)

    here = c * NE + j
    for src, dst, base in ((SX, X, S_A2X), (SD, D, S_A2D)):
        for k in range(1, NE):
            send(src.at[:, peer(k)], dst.at[:, here], base + k, {"expert": peer(k)})
    local = []
    for src, dst, base in ((SX, X, S_A2X), (SD, D, S_A2D)):
        copy = pltpu.make_async_copy(src.at[:, j], dst.at[:, here], rs.at[base])
        copy.start()
        local.append(copy)

    arrived(W.at[y, zm], S_AGZ)
    send(W.at[y, zm, low], W.at[y, zm, low], S_AGZ + 2, to_zp)
    along_y(1, zm)
    arrived(W.at[y, zp], S_AGZ + 1)
    send(W.at[y, zp, high], W.at[y, zp, high], S_AGZ + 3, to_zm)
    along_y(2, zp)
    onward_y(0, z)
    arrived(W.at[y, z2, low], S_AGZ + 2)
    arrived(W.at[y, z2, high], S_AGZ + 3)
    along_y(3, z2)

    for n, (dst, base) in enumerate(((X, S_A2X), (D, S_A2D))):
        local[n].wait()
        for k in range(1, NE):
            arrived(dst.at[:, c * NE + source(k)], base + k)
        own = dst.at[:, pl.ds(c * NE, NE)]
        send(own, own, S_SX + n, sib)
    onward_y(1, zm)
    onward_y(2, zp)
    arrived(X.at[:, pl.ds(o * NE, NE)], S_SX)
    arrived(D.at[:, pl.ds(o * NE, NE)], S_SX + 1)

    def turn(yy, carry):
        XT[yy] = X[yy].reshape(2 * ROWS, YB).T
        DT[yy] = D[yy].reshape(2 * ROWS, YB).T
        return carry

    lax.fori_loop(0, NY, turn, 0)

    def accumulate(yy, first):
        def tile(m, carry):
            rows = pl.ds(pl.multiple_of(m * ROWS, ROWS), ROWS)
            blocks = pl.ds(m * NE, NE)
            for ref, cols in ((X, (0, 256)), (X, (256, 512)), (X, (512, 768)), (D, (768, 1152))):
                lo, hi = cols
                got = jnp.dot(
                    ref[yy, blocks].reshape(ROWS, YB),
                    W[yy, :, :, lo:hi].reshape(YB, hi - lo),
                    preferred_element_type=F32,
                )
                if first:
                    ACC[rows, lo:hi] = got
                else:
                    ACC[rows, lo:hi] += got
            return carry

        lax.fori_loop(0, 2, tile, 0)

    accumulate(y, True)
    onward_y(3, z2)
    accumulate(ym, False)
    accumulate(yp, False)
    for step, zz in enumerate((z, zm, zp, z2)):
        arrived(W.at[y2, zz, low], S_AGY + 4 * step + 2)
        arrived(W.at[y2, zz, high], S_AGY + 4 * step + 3)
    accumulate(y2, False)

    def activate(m, carry):
        rows = pl.ds(pl.multiple_of(m * 64, 64), 64)
        gate, up, d_hidden = ACC[rows, 0:HH], ACC[rows, HH:2 * HH], ACC[rows, 2 * HH:HC]
        sig = jax.nn.sigmoid(gate)
        act = gate * sig
        CAT[rows, 0:HH] = (d_hidden * up * sig * (1.0 + gate * (1.0 - sig))).astype(BF16)
        CAT[rows, HH:2 * HH] = (d_hidden * act).astype(BF16)
        CAT[rows, 2 * HH:HC] = (act * up).astype(BF16)
        return carry

    lax.fori_loop(0, 2 * ROWS // 64, activate, 0)

    def partials(yy):
        for ref, lo, hi in ((XT, 0, 256), (XT, 256, 512), (XT, 512, 768), (DT, 768, 1152)):
            got = jnp.dot(ref[yy], CAT[:, lo:hi], preferred_element_type=F32)
            T[yy, :, :, lo:hi] = got.astype(BF16).reshape(NZ, SH, hi - lo)

    nt = (((1,), (1,)), ((), ()))

    def outputs(side, write):
        rows = pl.ds(pl.multiple_of(side * ROWS, ROWS), ROWS)

        def tile(yy, carry):
            out = lax.dot_general(
                CAT[rows, 2 * HH:HC], W[yy, :, :, 2 * HH:HC].reshape(YB, HH), nt,
                preferred_element_type=F32,
            )
            write(0, yy, out)
            d_in = lax.dot_general(
                CAT[rows, 0:2 * HH], W[yy, :, :, 0:2 * HH].reshape(YB, 2 * HH), nt,
                preferred_element_type=F32,
            )
            write(1, yy, d_in)
            return carry

        lax.fori_loop(0, NY, tile, 0)

    order = (z2, zp, zm, z)
    partials(y2)
    for step, zz in enumerate(order):
        send(T.at[y2, zz, low], R1.at[0, step], S_RY1 + 2 * step, to_yp)
        send(T.at[y2, zz, high], R1.at[1, step], S_RY1 + 2 * step + 1, to_ym)

    def write_sibling(n, yy, value):
        OS[n, yy] = value.astype(BF16).reshape(NE, CAP, YB)

    outputs(o, write_sibling)
    for n in range(2):
        send(OS.at[n], OR.at[n], S_SO + n, sib)
    partials(yp)
    partials(ym)

    def second_y(step, zz):
        arrived(R1.at[0, step], S_RY1 + 2 * step)
        T[yp, zz, 0:64] = (T[yp, zz, 0:64].astype(F32) + R1[0, step].astype(F32)).astype(BF16)
        send(T.at[yp, zz], R2.at[0, step], S_RY2 + 2 * step, to_yp)
        arrived(R1.at[1, step], S_RY1 + 2 * step + 1)
        T[ym, zz, 64:128] = (T[ym, zz, 64:128].astype(F32) + R1[1, step].astype(F32)).astype(BF16)
        send(T.at[ym, zz], R2.at[1, step], S_RY2 + 2 * step + 1, to_ym)

    second_y(0, order[0])

    for n in range(2):
        arrived(OR.at[n], S_SO + n)

    def write_own(n, yy, value):
        value = value + OR[n, yy].reshape(ROWS, YB).astype(F32)
        BS[n, yy] = value.astype(BF16).reshape(NE, CAP, YB)

    outputs(c, write_own)
    for n, base in ((0, S_BO), (1, S_BI)):
        for k in range(1, NE):
            send(BS.at[n, :, peer(k)], BK.at[n, :, j], base + k, {"expert": peer(k)})
    local = []
    for n, base in ((0, S_BO), (1, S_BI)):
        copy = pltpu.make_async_copy(BS.at[n, :, j], BK.at[n, :, j], rs.at[base])
        copy.start()
        local.append(copy)

    second_y(1, order[1])
    partials(y)
    second_y(2, order[2])
    second_y(3, order[3])

    def summed_y(step, zz):
        arrived(R2.at[0, step], S_RY2 + 2 * step)
        arrived(R2.at[1, step], S_RY2 + 2 * step + 1)
        return T[y, zz].astype(F32) + R2[0, step].astype(F32) + R2[1, step].astype(F32)

    ZS[0] = summed_y(0, z2).astype(BF16)
    send(ZS.at[0, low], Z1.at[0], S_RZ1, to_zp)
    send(ZS.at[0, high], Z1.at[1], S_RZ1 + 1, to_zm)

    total = summed_y(1, zp)
    arrived(Z1.at[0], S_RZ1)
    ZS[1, 0:64] = (total[0:64] + Z1[0].astype(F32)).astype(BF16)
    ZS[1, 64:128] = total[64:128].astype(BF16)
    send(ZS.at[1], Z2.at[0], S_RZ2, to_zp)

    total = summed_y(2, zm)
    arrived(Z1.at[1], S_RZ1 + 1)
    ZS[2, 0:64] = total[0:64].astype(BF16)
    ZS[2, 64:128] = (total[64:128] + Z1[1].astype(F32)).astype(BF16)
    send(ZS.at[2], Z2.at[1], S_RZ2 + 1, to_zm)

    for n, base in ((0, S_BO), (1, S_BI)):
        local[n].wait()
        for k in range(1, NE):
            arrived(BK.at[n, :, source(k)], base + k)
    for yy in range(NY):
        back = BK[0, yy].reshape(ROWS, YB)
        out = sum(jnp.dot(SEL[n], back, preferred_element_type=F32) for n in (3, 2, 1))
        back = BK[1, yy].reshape(ROWS, YB)
        d_in = jnp.dot(SEL[0], back, preferred_element_type=F32)
        for zz in range(NZ):
            cols = slice((zz * 4 + yy) * SH, (zz * 4 + yy + 1) * SH)
            lo_ref[:, cols] = out[:, zz * SH:(zz + 1) * SH].astype(BF16)
            dt_ref[:, cols] = d_in[:, zz * SH:(zz + 1) * SH].astype(BF16)

    total = summed_y(3, z)
    arrived(Z2.at[0], S_RZ2)
    arrived(Z2.at[1], S_RZ2 + 1)
    total = total + Z2[0].astype(F32) + Z2[1].astype(F32)
    FS[...] = total.reshape(2, 64, HC)
    send(FS.at[o], FR, S_FIN, sib)
    for n, ref in enumerate((gg_ref, gu_ref, gd_ref)):
        ref[0, :, half_c] = FS[c, :, n * HH:(n + 1) * HH]
    arrived(FR, S_FIN)
    for n, ref in enumerate((gg_ref, gu_ref, gd_ref)):
        ref[0, :, half_o] = FR[:, n * HH:(n + 1) * HH]

    for copy in sent:
        copy.wait_send()


def shards(tokens, routes, gate_scale, w_gate, w_up, w_down, d_out):
    vm = pl.BlockSpec(memory_space=pltpu.VMEM)
    grad = jax.ShapeDtypeStruct(w_gate.shape, F32)
    rows = jax.ShapeDtypeStruct(tokens.shape, BF16)
    return pl.pallas_call(
        kernel,
        out_shape=(rows, rows, grad, grad, grad),
        in_specs=[vm] * 7,
        out_specs=(vm,) * 5,
        scratch_shapes=[
            pltpu.VMEM((NY, NZ, SH, HC), BF16),
            pltpu.VMEM((NY, 2 * NE, CAP, YB), BF16),
            pltpu.VMEM((NY, 2 * NE, CAP, YB), BF16),
            pltpu.VMEM((NY, YB, 2 * ROWS), BF16),
            pltpu.VMEM((NY, YB, 2 * ROWS), BF16),
            pltpu.VMEM((NY, NE, CAP, YB), BF16),
            pltpu.VMEM((NY, NE, CAP, YB), BF16),
            pltpu.VMEM((4, TOK, ROWS), BF16),
            pltpu.VMEM((2 * ROWS, HC), F32),
            pltpu.VMEM((2 * ROWS, HC), BF16),
            pltpu.VMEM((NY, NZ, SH, HC), BF16),
            pltpu.VMEM((2, NZ, 64, HC), BF16),
            pltpu.VMEM((2, NZ, SH, HC), BF16),
            pltpu.VMEM((2, 64, HC), BF16),
            pltpu.VMEM((2, SH, HC), BF16),
            pltpu.VMEM((3, SH, HC), BF16),
            pltpu.VMEM((2, 64, HC), F32),
            pltpu.VMEM((64, HC), F32),
            pltpu.VMEM((2, NY, NE, CAP, YB), BF16),
            pltpu.VMEM((2, NY, NE, CAP, YB), BF16),
            pltpu.VMEM((2, NY, NE, CAP, YB), BF16),
            pltpu.VMEM((2, NY, NE, CAP, YB), BF16),
            pltpu.SemaphoreType.DMA((S_ALL,)),
            pltpu.SemaphoreType.DMA((S_ALL,)),
        ],
        compiler_params=pltpu.CompilerParams(
            collective_id=0, has_side_effects=True, vmem_limit_bytes=60 * 1024 * 1024
        ),
    )(tokens, routes, gate_scale, w_gate, w_up, w_down, d_out)


def solution(mesh):
    tok = P(("dp", "expert"), None)
    wei = P("expert", "dp", None)
    return jax.shard_map(
        shards,
        mesh=mesh,
        in_specs=(tok, tok, tok, wei, wei, wei, tok),
        out_specs=(tok, tok, wei, wei, wei),
        check_vma=False,
    )
```

time: 495 us -> 147 us (0.30)
  waiting for transfers between devices: 378 us -> 0 us
  Pallas kernels: 0 us -> 138 us
  matrix products: 29.4 us -> 0 us
  local copies, waits for them, and re-layouts: 33.9 us -> 8.19 us
  other arithmetic: 19.2 us -> 0 us
  starting transfers between devices: 18.4 us -> 0 us
  between operations: 14.4 us -> 0.66 us
    reduce_scatter x3 -> x0, waiting for transfers between devices: 208 us -> none  [the longest x1 95.8 us: shards(): lax.psum_scatter(term_gate.astype(jnp.bfloat16), 'dp', scatter_dimension=...]
    pallas_call x0 -> x1, Pallas kernels: none -> 138 us  [shards(): pl.pallas_call(kernel, out_shape=(rows, rows, grad, grad, grad), in_specs...]
    all_gather x3 -> x0, waiting for transfers between devices: 136 us -> none  [the longest x1 53.7 us: shards(): lax.all_gather(w_gate, 'dp', axis=1, tiled=True)]
    all_to_all x4 -> x0, waiting for transfers between devices: 31.7 us -> none  [the longest x1 12.8 us: shards(): lax.all_to_all(send_d, 'expert', split_axis=0, concat_axis=0, tiled=True)]
    dot_general x9 -> x0, matrix products: 29.4 us -> none  [the longest x1 4.27 us: shards(): gate = jnp.dot(rows_x, weight_gate, preferred_element_type=jnp.float32)]
    gather x14 -> x0, local copies, waits for them, and re-layouts: 28.2 us -> none  [the longest x6 12.3 us: shards(): back_out[rows_pick].astype(jnp.float32)]
    all_to_all x4 -> x0, starting transfers between devices: 18 us -> none  [the longest x1 6.33 us: shards(): lax.all_to_all(send_d, 'expert', split_axis=0, concat_axis=0, tiled=True)]
    convert_element_type x4 -> x0, other arithmetic: 7.28 us -> none  [the longest x1 4.11 us: shards(): d_tokens = total_in.astype(jnp.bfloat16)]
  transfers between devices with their start and end apart: 10 -> 0, of which waited for: 9 -> 0; matrix products, arithmetic and copies ran while one was open for 14% -> 0% of each run, Pallas kernels for 0% -> 0%
where the time goes in v1:
time: 147 us
  Pallas kernels  138 us (94%)
  local copies, waits for them, and re-layouts  8.19 us (6%)
    pallas_call x1, Pallas kernels, shards(): pl.pallas_call(kernel, out_shape=(rows, rows, grad, grad, grad), in_specs...  138 us
    unnamed x17, local copies, waits for them, and re-layouts  8.19 us

profile of v1, /device:TPU:1, one launch (start us, length us, event | category | flops | bytes accessed | tf_op | source)
XLA Modules:
  0.0 146.7 jit_solution(5994761649020217993)
XLA Ops:
  0.6 0.0 copy-start.4
  0.6 1.5 copy.12.rt_ref
  2.1 0.0 copy-done.4
  2.1 0.8 copy.13.gs_ref
  2.9 137.9 %shard_map.110 = (bf16[192,2048]{1,0:T(8,128)(2,1)}, bf16[192,2048]{1,0:T(8,128)(2,1)}, f32[1,64,768]{2,1,0:T(8,128)}, f32[1,64,768]{2,1,0:T(8,128)}, f32[1,64,768]{2,1,0:T(8,128)}) custom-call(bf16[192,2048]{1,0:T(8,128)(2,1)} %tok_ref.1, s32[192,6]{1,0:T(8,128)} %copy.12.rt_ref, f32[192,6]{1,0:T(8,128)} %copy.13.gs_ref, bf16[1,64,768]{2,1,0:T(8,128)(2,1)} %wg_ref.1, ...), custom_call_target="tpu_custom_call" | custom-call | tf_op jit(solution)/shard_map/pallas_call | solution.py:376
  140.8 0.0 copy-start
  140.8 2.2 %copy.19 = bf16[192,2048]{1,0:T(8,128)(2,1)} copy(bf16[192,2048]{1,0:T(8,128)(2,1)} %get-tuple-element.10) | data formatting | bytes 1572864
  142.9 0.0 copy-done
  142.9 0.0 copy-start.3
  142.9 0.9 copy.20
  143.8 0.2 copy-done.3
  144.1 0.0 copy-start.2
  144.1 0.7 copy.21
  144.7 0.3 copy-done.2
  145.1 0.0 copy-start.1
  145.1 0.7 copy.22
  145.7 0.3 copy-done.1
  146.1 0.7 copy.23
Async XLA Ops:
  0.6 1.5 %copy-start.4 = (f32[192,6]{0,1:T(8,128)S(1)}, f32[192,6]{0,1:T(8,128)}, u32[]{:S(2)}) copy-start(f32[192,6]{0,1:T(8,128)} %param.9) | copy-start | bytes 13828
  140.8 2.2 %copy-start = (bf16[192,2048]{1,0:T(8,128)(2,1)S(1)}, bf16[192,2048]{1,0:T(8,128)(2,1)}, u32[]{:S(2)}) copy-start(bf16[192,2048]{1,0:T(8,128)(2,1)} %get-tuple-element.11) | copy-start | bytes 2359300
  142.9 1.1 copy-start.3
  144.1 1.0 copy-start.2
  145.1 1.0 copy-start.1

commit v2 on v1

--- a/solution.py
+++ b/solution.py
@@ -18,22 +18,7 @@
 TOK = 192
 ROWS = NE * CAP
 
-S_SIB = 0
-S_LOC = 3
-S_AGZ = 6
-S_AGY = 10
-S_A2X = 26
-S_A2D = 34
-S_SX = 42
-S_SO = 44
-S_BO = 46
-S_BI = 54
-S_RY1 = 62
-S_RY2 = 70
-S_RZ1 = 78
-S_RZ2 = 80
-S_FIN = 82
-S_ALL = 83
+N_SEM = 128
 
 
 def kernel(
@@ -49,25 +34,40 @@
     p = lax.div(i, 2)
     y = lax.rem(p, 4)
     z = lax.div(p, 4)
+    x = lax.div(j, 2)
+    side = lax.rem(j, 2)
     yp, ym, y2 = lax.rem(y + 1, 4), lax.rem(y + 3, 4), lax.rem(y + 2, 4)
     zp, zm, z2 = lax.rem(z + 1, 4), lax.rem(z + 3, 4), lax.rem(z + 2, 4)
+    zn = lax.rem(z + 3 + 2 * side, 4)
 
     def place(yy, zz, cc):
         return {"dp": (zz * 4 + yy) * 2 + cc}
 
     sib = place(y, z, o)
-    to_yp, to_ym = place(yp, z, c), place(ym, z, c)
-    to_zp, to_zm = place(y, zp, c), place(y, zm, c)
-
-    def peer(k):
-        return lax.rem(j + k, NE)
-
-    def source(k):
-        return lax.rem(j + NE - k, NE)
+    up_y, down_y = place(yp, z, c), place(ym, z, c)
+    up_z, down_z = place(y, zp, c), place(y, zm, c)
+
+    near, far = pl.ds(0, 16), pl.ds(16, 16)
+
+    def partners(q):
+        to, fro = lax.rem(x + q, 4), lax.rem(x + 4 - q, 4)
+        across = [
+            (near, to * 2 + 1 - side, fro * 2 + 1 - side, {"expert": to * 2 + 1 - side}),
+            (far, to * 2 + 1 - side, fro * 2 + 1 - side,
+             {"dp": (zn * 4 + y) * 2 + c, "expert": to * 2 + 1 - side}),
+        ]
+        same = [(pl.ds(0, CAP), to * 2 + side, fro * 2 + side, {"expert": to * 2 + side})]
+        return same if q else [], across
+
+    numbers = {}
+
+    def number(*name):
+        return numbers.setdefault(name, len(numbers))
 
     sent = []
 
-    def send(src, dst, k, to):
+    def send(src, dst, name, to):
+        k = number(*name)
         copy = pltpu.make_async_remote_copy(
             src_ref=src, dst_ref=dst, send_sem=ss.at[k], recv_sem=rs.at[k],
             device_id=to, device_id_type=MESH,
@@ -75,52 +75,54 @@
         copy.start()
         sent.append(copy)
 
-    def arrived(ref, k, to=None):
+    def arrived(ref, *name):
+        k = number(*name)
         pltpu.make_async_remote_copy(
             src_ref=ref, dst_ref=ref, send_sem=ss.at[k], recv_sem=rs.at[k],
-            device_id=sib if to is None else to, device_id_type=MESH,
+            device_id=sib, device_id_type=MESH,
         ).wait_recv()
 
     barrier = pltpu.get_barrier_semaphore()
-    for to in (sib, to_yp, to_ym, to_zp, to_zm):
+    greet = [sib, up_y, down_y, up_z, down_z]
+    for q in range(4):
+        same, across = partners(q)
+        greet += [to for _, _, _, to in same + across]
+    for to in greet:
         pl.semaphore_signal(barrier, inc=1, device_id=to, device_id_type=MESH)
-    for k in range(1, NE):
-        pl.semaphore_signal(barrier, inc=1, device_id={"expert": peer(k)}, device_id_type=MESH)
-    pl.semaphore_wait(barrier, 5 + NE - 1)
-
-    mine = pl.ds(pl.multiple_of(c * 64, 64), 64)
-    theirs = pl.ds(pl.multiple_of(o * 64, 64), 64)
+    pl.semaphore_wait(barrier, len(greet))
+
+    f = pl.ds(pl.multiple_of(c * 64, 64), 64)
+    g = pl.ds(pl.multiple_of(o * 64, 64), 64)
     half_c = pl.ds(pl.multiple_of(c * HH, 128), HH)
     half_o = pl.ds(pl.multiple_of(o * HH, 128), HH)
     local = []
     for n, w_ref in enumerate((wg_ref, wu_ref, wd_ref)):
         cols = pl.ds(n * HH, HH)
-        send(w_ref.at[0, :, half_o], W.at[y, z, mine, cols], S_SIB + n, sib)
+        send(w_ref.at[0, :, half_o], W.at[y, z, f, cols], ("sib", n), sib)
         copy = pltpu.make_async_copy(
-            w_ref.at[0, :, half_c], W.at[y, z, mine, cols], rs.at[S_LOC + n]
+            w_ref.at[0, :, half_c], W.at[y, z, f, cols], rs.at[number("own", n)]
         )
         copy.start()
         local.append(copy)
     for copy in local:
         copy.wait()
+
+    def along(yy, zz, piece, name, to):
+        send(W.at[yy, zz, piece], W.at[yy, zz, piece], name, to)
+
+    def here(yy, zz, piece, *name):
+        arrived(W.at[yy, zz, piece], *name)
+
+    along(y, z, f, ("gz", "f", "up"), up_z)
+    along(y, z, f, ("gy", 0, "f", "up"), up_y)
     for n in range(3):
-        arrived(W.at[y, z, theirs, pl.ds(n * HH, HH)], S_SIB + n)
-
-    low, high = pl.ds(0, 64), pl.ds(64, 64)
-
-    def along_y(step, zz):
-        send(W.at[y, zz], W.at[y, zz], S_AGY + 4 * step, to_yp)
-        send(W.at[y, zz], W.at[y, zz], S_AGY + 4 * step + 1, to_ym)
-
-    def onward_y(step, zz):
-        arrived(W.at[ym, zz], S_AGY + 4 * step)
-        send(W.at[ym, zz, low], W.at[ym, zz, low], S_AGY + 4 * step + 2, to_yp)
-        arrived(W.at[yp, zz], S_AGY + 4 * step + 1)
-        send(W.at[yp, zz, high], W.at[yp, zz, high], S_AGY + 4 * step + 3, to_ym)
-
-    send(W.at[y, z], W.at[y, z], S_AGZ, to_zp)
-    send(W.at[y, z], W.at[y, z], S_AGZ + 1, to_zm)
-    along_y(0, z)
+        arrived(W.at[y, z, g, pl.ds(n * HH, HH)], "sib", n)
+    along(y, z, g, ("gz", "g", "down"), down_z)
+    along(y, z, g, ("gy", 0, "g", "down"), down_y)
+    along(y, z, g, ("gz", "g", "up"), up_z)
+    along(y, z, g, ("gy", 0, "g", "up"), up_y)
+    along(y, z, f, ("gz", "f", "down"), down_z)
+    along(y, z, f, ("gy", 0, "f", "down"), down_y)
 
     shape = (TOK, ROWS)
     lane = lax.broadcasted_iota(jnp.int32, shape, 1)
@@ -166,38 +168,70 @@
         SX[yy] = rows.astype(BF16).reshape(NE, CAP, YB)
         rows = lax.dot_general(SEL[0], columns(do_ref, yy), tn, preferred_element_type=F32)
         SD[yy] = (rows * slot_weight).astype(BF16).reshape(NE, CAP, YB)
-
-    here = c * NE + j
-    for src, dst, base in ((SX, X, S_A2X), (SD, D, S_A2D)):
-        for k in range(1, NE):
-            send(src.at[:, peer(k)], dst.at[:, here], base + k, {"expert": peer(k)})
+    mine = c * NE + j
+    rows_out = ((SX, X, "x"), (SD, D, "d"))
+
+    def exchange(crossing):
+        for src, dst, what in rows_out:
+            for q in range(4):
+                for rows, to, _, device in partners(q)[crossing]:
+                    which = 0 if rows is near else 1
+                    send(src.at[:, to, rows], dst.at[:, mine, rows],
+                         ("to", what, crossing, q, which), device)
+
+    exchange(0)
     local = []
-    for src, dst, base in ((SX, X, S_A2X), (SD, D, S_A2D)):
-        copy = pltpu.make_async_copy(src.at[:, j], dst.at[:, here], rs.at[base])
+    for src, dst, what in rows_out:
+        copy = pltpu.make_async_copy(src.at[:, j], dst.at[:, mine], rs.at[number("keep", what)])
         copy.start()
         local.append(copy)
 
-    arrived(W.at[y, zm], S_AGZ)
-    send(W.at[y, zm, low], W.at[y, zm, low], S_AGZ + 2, to_zp)
-    along_y(1, zm)
-    arrived(W.at[y, zp], S_AGZ + 1)
-    send(W.at[y, zp, high], W.at[y, zp, high], S_AGZ + 3, to_zm)
-    along_y(2, zp)
-    onward_y(0, z)
-    arrived(W.at[y, z2, low], S_AGZ + 2)
-    arrived(W.at[y, z2, high], S_AGZ + 3)
-    along_y(3, z2)
-
-    for n, (dst, base) in enumerate(((X, S_A2X), (D, S_A2D))):
+    def spread_y(step, zz, piece, kind):
+        along(y, zz, piece, ("gy", step, kind, "up"), up_y)
+        along(y, zz, piece, ("gy", step, kind, "down"), down_y)
+
+    def onward_f(step, zz):
+        here(ym, zz, f, "gy", step, "f", "up")
+        along(ym, zz, f, ("gy", step, "f", "on"), up_y)
+
+    def onward_g(step, zz):
+        here(yp, zz, g, "gy", step, "g", "down")
+        along(yp, zz, g, ("gy", step, "g", "on"), down_y)
+
+    here(y, zm, f, "gz", "f", "up")
+    along(y, zm, f, ("gz", "f", "on"), up_z)
+    spread_y(1, zm, f, "f")
+    here(y, zp, g, "gz", "g", "down")
+    along(y, zp, g, ("gz", "g", "on"), down_z)
+    spread_y(2, zp, g, "g")
+    exchange(1)
+    onward_f(0, z)
+    onward_g(0, z)
+    here(y, zm, g, "gz", "g", "up")
+    spread_y(1, zm, g, "g")
+    here(y, zp, f, "gz", "f", "down")
+    spread_y(2, zp, f, "f")
+    onward_f(1, zm)
+    onward_g(2, zp)
+    here(y, z2, f, "gz", "f", "on")
+    spread_y(3, z2, f, "f")
+    here(y, z2, g, "gz", "g", "on")
+    spread_y(3, z2, g, "g")
+    onward_g(1, zm)
+    onward_f(2, zp)
+    for n, (_, dst, what) in enumerate(rows_out):
         local[n].wait()
-        for k in range(1, NE):
-            arrived(dst.at[:, c * NE + source(k)], base + k)
+        for q in range(4):
+            for crossing in range(2):
+                for rows, _, fro, _ in partners(q)[crossing]:
+                    which = 0 if rows is near else 1
+                    arrived(dst.at[:, c * NE + fro, rows], "to", what, crossing, q, which)
         own = dst.at[:, pl.ds(c * NE, NE)]
-        send(own, own, S_SX + n, sib)
-    onward_y(1, zm)
-    onward_y(2, zp)
-    arrived(X.at[:, pl.ds(o * NE, NE)], S_SX)
-    arrived(D.at[:, pl.ds(o * NE, NE)], S_SX + 1)
+        send(own, own, ("rows", what), sib)
+    onward_f(3, z2)
+    onward_g(3, z2)
+    arrived(X.at[:, pl.ds(o * NE, NE)], "rows", "x")
+    arrived(D.at[:, pl.ds(o * NE, NE)], "rows", "d")
 
     def turn(yy, carry):
         XT[yy] = X[yy].reshape(2 * ROWS, YB).T
@@ -224,14 +258,17 @@
             return carry
 
         lax.fori_loop(0, 2, tile, 0)
-
     accumulate(y, True)
-    onward_y(3, z2)
+    steps = ((0, z), (1, zm), (2, zp), (3, z2))
+    for step, zz in steps:
+        here(ym, zz, g, "gy", step, "g", "up")
     accumulate(ym, False)
+    for step, zz in steps:
+        here(yp, zz, f, "gy", step, "f", "down")
     accumulate(yp, False)
-    for step, zz in enumerate((z, zm, zp, z2)):
-        arrived(W.at[y2, zz, low], S_AGY + 4 * step + 2)
-        arrived(W.at[y2, zz, high], S_AGY + 4 * step + 3)
+    for step, zz in steps:
+        here(y2, zz, f, "gy", step, "f", "on")
+        here(y2, zz, g, "gy", step, "g", "on")
     accumulate(y2, False)
 
     def activate(m, carry):
@@ -271,78 +308,97 @@
 
         lax.fori_loop(0, NY, tile, 0)
 
-    order = (z2, zp, zm, z)
+    def first_y(step, zz):
+        send(T.at[y2, zz, f], R1.at[0, step], ("r1", step, "f"), up_y)
+        send(T.at[y2, zz, g], R1.at[1, step], ("r1", step, "g"), down_y)
+
+    def second_y(step, zz):
+        send(T.at[yp, zz, g], R2.at[0, step, g], ("r2", step, "g", "up"), up_y)
+        send(T.at[ym, zz, f], R2.at[1, step, f], ("r2", step, "f", "down"), down_y)
+
+    def third_y(step, zz):
+        arrived(R1.at[0, step], "r1", step, "f")
+        T[yp, zz, f] = (T[yp, zz, f].astype(F32) + R1[0, step].astype(F32)).astype(BF16)
+        send(T.at[yp, zz, f], R2.at[0, step, f], ("r2", step, "f", "up"), up_y)
+        arrived(R1.at[1, step], "r1", step, "g")
+        T[ym, zz, g] = (T[ym, zz, g].astype(F32) + R1[1, step].astype(F32)).astype(BF16)
+        send(T.at[ym, zz, g], R2.at[1, step, g], ("r2", step, "g", "down"), down_y)
+
     partials(y2)
-    for step, zz in enumerate(order):
-        send(T.at[y2, zz, low], R1.at[0, step], S_RY1 + 2 * step, to_yp)
-        send(T.at[y2, zz, high], R1.at[1, step], S_RY1 + 2 * step + 1, to_ym)
+    first_y(0, z2)
+    partials(yp)
+    partials(ym)
+    second_y(0, z2)
+    first_y(1, zp)
 
     def write_sibling(n, yy, value):
         OS[n, yy] = value.astype(BF16).reshape(NE, CAP, YB)
 
     outputs(o, write_sibling)
     for n in range(2):
-        send(OS.at[n], OR.at[n], S_SO + n, sib)
-    partials(yp)
-    partials(ym)
-
-    def second_y(step, zz):
-        arrived(R1.at[0, step], S_RY1 + 2 * step)
-        T[yp, zz, 0:64] = (T[yp, zz, 0:64].astype(F32) + R1[0, step].astype(F32)).astype(BF16)
-        send(T.at[yp, zz], R2.at[0, step], S_RY2 + 2 * step, to_yp)
-        arrived(R1.at[1, step], S_RY1 + 2 * step + 1)
-        T[ym, zz, 64:128] = (T[ym, zz, 64:128].astype(F32) + R1[1, step].astype(F32)).astype(BF16)
-        send(T.at[ym, zz], R2.at[1, step], S_RY2 + 2 * step + 1, to_ym)
-
-    second_y(0, order[0])
+        send(OS.at[n], OR.at[n], ("part", n), sib)
+    third_y(0, z2)
+    first_y(2, zm)
+    second_y(1, zp)
+    second_y(2, zm)
 
     for n in range(2):
-        arrived(OR.at[n], S_SO + n)
+        arrived(OR.at[n], "part", n)
 
     def write_own(n, yy, value):
         value = value + OR[n, yy].reshape(ROWS, YB).astype(F32)
         BS[n, yy] = value.astype(BF16).reshape(NE, CAP, YB)
 
     outputs(c, write_own)
-    for n, base in ((0, S_BO), (1, S_BI)):
-        for k in range(1, NE):
-            send(BS.at[n, :, peer(k)], BK.at[n, :, j], base + k, {"expert": peer(k)})
+    for crossing in (1, 0):
+        for n in range(2):
+            for q in range(4):
+                for rows, to, _, device in partners(q)[crossing]:
+                    which = 0 if rows is near else 1
+                    send(BS.at[n, :, to, rows], BK.at[n, :, j, rows],
+                         ("back", n, crossing, q, which), device)
     local = []
-    for n, base in ((0, S_BO), (1, S_BI)):
-        copy = pltpu.make_async_copy(BS.at[n, :, j], BK.at[n, :, j], rs.at[base])
+    for n in range(2):
+        copy = pltpu.make_async_copy(BS.at[n, :, j], BK.at[n, :, j], rs.at[number("stay", n)])
         copy.start()
         local.append(copy)
 
-    second_y(1, order[1])
+    third_y(1, zp)
+    first_y(3, z)
+    third_y(2, zm)
+    second_y(3, z)
     partials(y)
-    second_y(2, order[2])
-    second_y(3, order[3])
 
     def summed_y(step, zz):
-        arrived(R2.at[0, step], S_RY2 + 2 * step)
-        arrived(R2.at[1, step], S_RY2 + 2 * step + 1)
+        for d in range(2):
+            for piece, kind in ((f, "f"), (g, "g")):
+                arrived(R2.at[d, step, piece], "r2", step, kind, ("up", "down")[d])
         return T[y, zz].astype(F32) + R2[0, step].astype(F32) + R2[1, step].astype(F32)
 
     ZS[0] = summed_y(0, z2).astype(BF16)
-    send(ZS.at[0, low], Z1.at[0], S_RZ1, to_zp)
-    send(ZS.at[0, high], Z1.at[1], S_RZ1 + 1, to_zm)
-
-    total = summed_y(1, zp)
-    arrived(Z1.at[0], S_RZ1)
-    ZS[1, 0:64] = (total[0:64] + Z1[0].astype(F32)).astype(BF16)
-    ZS[1, 64:128] = total[64:128].astype(BF16)
-    send(ZS.at[1], Z2.at[0], S_RZ2, to_zp)
-
-    total = summed_y(2, zm)
-    arrived(Z1.at[1], S_RZ1 + 1)
-    ZS[2, 0:64] = total[0:64].astype(BF16)
-    ZS[2, 64:128] = (total[64:128] + Z1[1].astype(F32)).astype(BF16)
-    send(ZS.at[2], Z2.at[1], S_RZ2 + 1, to_zm)
-
-    for n, base in ((0, S_BO), (1, S_BI)):
+    send(ZS.at[0, f], Z1.at[0], ("z1", "f"), up_z)
+    send(ZS.at[0, g], Z1.at[1], ("z1", "g"), down_z)
+    third_y(3, z)
+
+    def second_z(n, zz, late, early, name, to):
+        FS[...] = summed_y(n, zz).reshape(2, 64, HC)
+        (piece, at), (first, first_at) = late, early
+        ZS[n, first] = FS[first_at].astype(BF16)
+        send(ZS.at[n, first], Z2.at[n - 1, first], ("z2", n, 0), to)
+        arrived(Z1.at[n - 1], "z1", name)
+        ZS[n, piece] = (FS[at] + Z1[n - 1].astype(F32)).astype(BF16)
+        send(ZS.at[n, piece], Z2.at[n - 1, piece], ("z2", n, 1), to)
+
+    second_z(1, zp, (f, c), (g, o), "f", up_z)
+    second_z(2, zm, (g, o), (f, c), "g", down_z)
+
+    for n in range(2):
         local[n].wait()
-        for k in range(1, NE):
-            arrived(BK.at[n, :, source(k)], base + k)
+        for q in range(4):
+            for crossing in range(2):
+                for rows, _, fro, _ in partners(q)[crossing]:
+                    which = 0 if rows is near else 1
+                    arrived(BK.at[n, :, fro, rows], "back", n, crossing, q, which)
     for yy in range(NY):
         back = BK[0, yy].reshape(ROWS, YB)
         out = sum(jnp.dot(SEL[n], back, preferred_element_type=F32) for n in (3, 2, 1))
@@ -352,21 +408,23 @@
             cols = slice((zz * 4 + yy) * SH, (zz * 4 + yy + 1) * SH)
             lo_ref[:, cols] = out[:, zz * SH:(zz + 1) * SH].astype(BF16)
             dt_ref[:, cols] = d_in[:, zz * SH:(zz + 1) * SH].astype(BF16)
-
     total = summed_y(3, z)
-    arrived(Z2.at[0], S_RZ2)
-    arrived(Z2.at[1], S_RZ2 + 1)
+    arrived(Z2.at[0, g], "z2", 1, 0)
+    arrived(Z2.at[0, f], "z2", 1, 1)
+    arrived(Z2.at[1, f], "z2", 2, 0)
+    arrived(Z2.at[1, g], "z2", 2, 1)
     total = total + Z2[0].astype(F32) + Z2[1].astype(F32)
     FS[...] = total.reshape(2, 64, HC)
-    send(FS.at[o], FR, S_FIN, sib)
+    send(FS.at[o], FR, ("fin",), sib)
     for n, ref in enumerate((gg_ref, gu_ref, gd_ref)):
         ref[0, :, half_c] = FS[c, :, n * HH:(n + 1) * HH]
-    arrived(FR, S_FIN)
+    arrived(FR, "fin")
     for n, ref in enumerate((gg_ref, gu_ref, gd_ref)):
         ref[0, :, half_o] = FR[:, n * HH:(n + 1) * HH]
 
     for copy in sent:
         copy.wait_send()
+    assert len(numbers) <= N_SEM
 
 
 def shards(tokens, routes, gate_scale, w_gate, w_up, w_down, d_out):
@@ -401,8 +459,8 @@
             pltpu.VMEM((2, NY, NE, CAP, YB), BF16),
             pltpu.VMEM((2, NY, NE, CAP, YB), BF16),
             pltpu.VMEM((2, NY, NE, CAP, YB), BF16),
-            pltpu.SemaphoreType.DMA((S_ALL,)),
-            pltpu.SemaphoreType.DMA((S_ALL,)),
+            pltpu.SemaphoreType.DMA((N_SEM,)),
+            pltpu.SemaphoreType.DMA((N_SEM,)),
         ],
         compiler_params=pltpu.CompilerParams(
             collective_id=0, has_side_effects=True, vmem_limit_bytes=60 * 1024 * 1024

time: 147 us -> 119 us (0.81)
  Pallas kernels: 138 us -> 110 us
    pallas_call x1, Pallas kernels: 138 us -> 110 us  [shards(): pl.pallas_call(kernel, out_shape=(rows, rows, grad, grad, grad), in_specs...]
where the time goes in v2:
time: 119 us
  Pallas kernels  110 us (92%)
  local copies, waits for them, and re-layouts  8.19 us (7%)
    pallas_call x1, Pallas kernels, shards(): pl.pallas_call(kernel, out_shape=(rows, rows, grad, grad, grad), in_specs...  110 us
    unnamed x17, local copies, waits for them, and re-layouts  8.19 us

profile of v2, /device:TPU:1, one launch (start us, length us, event | category | flops | bytes accessed | tf_op | source)
XLA Modules:
  0.0 118.6 jit_solution(3014226025700696328)
XLA Ops:
  0.6 0.0 copy-start.4
  0.6 1.5 %copy.12.rt_ref = s32[192,6]{1,0:T(8,128)} copy(s32[192,6]{0,1:T(8,128)} %param.8) | data formatting | bytes 9216 | tf_op args[1]
  2.1 0.0 copy-done.4
  2.1 0.8 copy.13.gs_ref
  2.9 109.8 %shard_map.110 = (bf16[192,2048]{1,0:T(8,128)(2,1)}, bf16[192,2048]{1,0:T(8,128)(2,1)}, f32[1,64,768]{2,1,0:T(8,128)}, f32[1,64,768]{2,1,0:T(8,128)}, f32[1,64,768]{2,1,0:T(8,128)}) custom-call(bf16[192,2048]{1,0:T(8,128)(2,1)} %tok_ref.1, s32[192,6]{1,0:T(8,128)} %copy.12.rt_ref, f32[192,6]{1,0:T(8,128)} %copy.13.gs_ref, bf16[1,64,768]{2,1,0:T(8,128)(2,1)} %wg_ref.1, ...), custom_call_target="tpu_custom_call" | custom-call | tf_op jit(solution)/shard_map/pallas_call | solution.py:434
  112.7 0.0 copy-start
  112.7 2.2 %copy.19 = bf16[192,2048]{1,0:T(8,128)(2,1)} copy(bf16[192,2048]{1,0:T(8,128)(2,1)} %get-tuple-element.10) | data formatting | bytes 1572864
  114.8 0.0 copy-done
  114.8 0.0 copy-start.3
  114.9 0.9 copy.20
  115.7 0.2 copy-done.3
  116.0 0.0 copy-start.2
  116.0 0.7 copy.21
  116.6 0.3 copy-done.2
  117.0 0.0 copy-start.1
  117.0 0.7 copy.22
  117.6 0.3 copy-done.1
  118.0 0.7 copy.23
Async XLA Ops:
  0.6 1.5 %copy-start.4 = (f32[192,6]{0,1:T(8,128)S(1)}, f32[192,6]{0,1:T(8,128)}, u32[]{:S(2)}) copy-start(f32[192,6]{0,1:T(8,128)} %param.9) | copy-start | bytes 13828
  112.7 2.2 %copy-start = (bf16[192,2048]{1,0:T(8,128)(2,1)S(1)}, bf16[192,2048]{1,0:T(8,128)(2,1)}, u32[]{:S(2)}) copy-start(bf16[192,2048]{1,0:T(8,128)(2,1)} %get-tuple-element.11) | copy-start | bytes 2359300
  114.8 1.1 copy-start.3
  116.0 1.0 copy-start.2
  117.0 1.0 copy-start.1

commit v3 on v2

--- a/solution.py
+++ b/solution.py
@@ -19,13 +19,14 @@
 ROWS = NE * CAP
 
 N_SEM = 128
+VMEM_MB = 50
 
 
 def kernel(
-    tok_ref, rt_ref, gs_ref, wg_ref, wu_ref, wd_ref, do_ref,
+    tok_hbm, rt_hbm, gs_hbm, wg_ref, wu_ref, wd_ref, do_hbm,
     lo_ref, dt_ref, gg_ref, gu_ref, gd_ref,
     W, X, D, XT, DT, SX, SD, SEL, ACC, CAT, T, R1, R2, Z1, Z2, ZS, FS, FR,
-    OS, OR, BS, BK, ss, rs,
+    OS, OR, BS, BK, tok_ref, do_ref, rt_ref, gs_ref, ss, rs,
 ):
     i = lax.axis_index("dp")
     j = lax.axis_index("expert")
@@ -82,6 +83,13 @@
             device_id=sib, device_id_type=MESH,
         ).wait_recv()
 
+    loads = []
+    for src, dst, what in (
+        (rt_hbm, rt_ref, "r"), (gs_hbm, gs_ref, "s"), (tok_hbm, tok_ref, "x"), (do_hbm, do_ref, "d")
+    ):
+        copy = pltpu.make_async_copy(src, dst, rs.at[number("load", what)])
+        copy.start()
+        loads.append(copy)
     barrier = pltpu.get_barrier_semaphore()
     greet = [sib, up_y, down_y, up_z, down_z]
     for q in range(4):
@@ -124,50 +132,50 @@
     along(y, z, f, ("gz", "f", "down"), down_z)
     along(y, z, f, ("gy", 0, "f", "down"), down_y)
 
-    shape = (TOK, ROWS)
-    lane = lax.broadcasted_iota(jnp.int32, shape, 1)
-    lane_e = lax.div(lane, CAP)
-    lane_s = lax.rem(lane, CAP).astype(F32)
+    shape = (ROWS, TOK)
+    row = lax.broadcasted_iota(jnp.int32, shape, 0)
+    row_e = lax.div(row, CAP)
+    row_s = lax.rem(row, CAP).astype(F32)
+    for copy in loads[:2]:
+        copy.wait()
     scale = gs_ref[...]
-    combine = scale / jnp.sum(scale, axis=1, keepdims=True)
+    combine = scale / jnp.sum(scale, axis=0, keepdims=True)
     routes = rt_ref[...]
     named = jnp.zeros(shape, F32)
     weight = jnp.zeros(shape, F32)
     for s in range(6):
-        same = routes[:, s:s + 1] == lane_e
+        same = routes[s:s + 1, :] == row_e
         named = jnp.where(same, 1.0, named)
-        weight = jnp.where(same, combine[:, s:s + 1], weight)
+        weight = jnp.where(same, combine[s:s + 1, :], weight)
     earlier = (
-        lax.broadcasted_iota(jnp.int32, (TOK, TOK), 1)
-        < lax.broadcasted_iota(jnp.int32, (TOK, TOK), 0)
+        lax.broadcasted_iota(jnp.int32, (TOK, TOK), 0)
+        < lax.broadcasted_iota(jnp.int32, (TOK, TOK), 1)
     ).astype(F32).astype(BF16)
-    position = jnp.dot(earlier, named.astype(BF16), preferred_element_type=F32)
-    chosen = jnp.where(position == lane_s, named, 0.0)
+    position = jnp.dot(named.astype(BF16), earlier, preferred_element_type=F32)
+    chosen = jnp.where(position == row_s, named, 0.0)
     weight = weight * chosen
-    SEL[0] = chosen.astype(BF16)
+    slot_weight = jnp.sum(weight, axis=1, keepdims=True)
+    select = chosen.astype(BF16)
+    SEL[0] = select
     rest = weight
     for n in range(1, 4):
         part = rest.astype(BF16)
         SEL[n] = part
         rest = rest - part.astype(F32)
 
-    tn = (((0,), (0,)), ((), ()))
-    ones = jnp.ones((TOK, 128), BF16)
-    slot_weight = sum(
-        lax.dot_general(SEL[n], ones, tn, preferred_element_type=F32) for n in (3, 2, 1)
-    )
-    slot_weight = jnp.concatenate([slot_weight] * 4, axis=1)
-
     def columns(ref, yy):
         return jnp.concatenate(
             [ref[:, (zz * 4 + yy) * SH:(zz * 4 + yy + 1) * SH] for zz in range(NZ)], axis=1
         )
 
+    for copy in loads[2:]:
+        copy.wait()
     for yy in range(NY):
-        rows = lax.dot_general(SEL[0], columns(tok_ref, yy), tn, preferred_element_type=F32)
+        rows = jnp.dot(select, columns(tok_ref, yy), preferred_element_type=F32)
         SX[yy] = rows.astype(BF16).reshape(NE, CAP, YB)
-        rows = lax.dot_general(SEL[0], columns(do_ref, yy), tn, preferred_element_type=F32)
+        rows = jnp.dot(select, columns(do_ref, yy), preferred_element_type=F32)
         SD[yy] = (rows * slot_weight).astype(BF16).reshape(NE, CAP, YB)
+
     mine = c * NE + j
     rows_out = ((SX, X, "x"), (SD, D, "d"))
 
@@ -230,46 +238,50 @@
         send(own, own, ("rows", what), sib)
     onward_f(3, z2)
     onward_g(3, z2)
+    def turn(m):
+        def body(yy, carry):
+            cols = pl.ds(pl.multiple_of(m * ROWS, ROWS), ROWS)
+            blocks = pl.ds(m * NE, NE)
+            XT[yy, :, cols] = X[yy, blocks].reshape(ROWS, YB).T
+            DT[yy, :, cols] = D[yy, blocks].reshape(ROWS, YB).T
+            return carry
+
+        lax.fori_loop(0, NY, body, 0)
+
+    def accumulate(yy, m, first):
+        rows = pl.ds(pl.multiple_of(m * ROWS, ROWS), ROWS)
+        blocks = pl.ds(m * NE, NE)
+        for ref, lo, hi in ((X, 0, 256), (X, 256, 512), (X, 512, 768), (D, 768, 1152)):
+            got = jnp.dot(
+                ref[yy, blocks].reshape(ROWS, YB),
+                W[yy, :, :, lo:hi].reshape(YB, hi - lo),
+                preferred_element_type=F32,
+            )
+            if first:
+                ACC[rows, lo:hi] = got
+            else:
+                ACC[rows, lo:hi] += got
+
+    steps = ((0, z), (1, zm), (2, zp), (3, z2))
+    turn(c)
+    accumulate(y, c, True)
+    for step, zz in steps:
+        here(ym, zz, g, "gy", step, "g", "up")
+    accumulate(ym, c, False)
+    for step, zz in steps:
+        here(yp, zz, f, "gy", step, "f", "down")
+    accumulate(yp, c, False)
     arrived(X.at[:, pl.ds(o * NE, NE)], "rows", "x")
     arrived(D.at[:, pl.ds(o * NE, NE)], "rows", "d")
-
-    def turn(yy, carry):
-        XT[yy] = X[yy].reshape(2 * ROWS, YB).T
-        DT[yy] = D[yy].reshape(2 * ROWS, YB).T
-        return carry
-
-    lax.fori_loop(0, NY, turn, 0)
-
-    def accumulate(yy, first):
-        def tile(m, carry):
-            rows = pl.ds(pl.multiple_of(m * ROWS, ROWS), ROWS)
-            blocks = pl.ds(m * NE, NE)
-            for ref, cols in ((X, (0, 256)), (X, (256, 512)), (X, (512, 768)), (D, (768, 1152))):
-                lo, hi = cols
-                got = jnp.dot(
-                    ref[yy, blocks].reshape(ROWS, YB),
-                    W[yy, :, :, lo:hi].reshape(YB, hi - lo),
-                    preferred_element_type=F32,
-                )
-                if first:
-                    ACC[rows, lo:hi] = got
-                else:
-                    ACC[rows, lo:hi] += got
-            return carry
-
-        lax.fori_loop(0, 2, tile, 0)
-    accumulate(y, True)
-    steps = ((0, z), (1, zm), (2, zp), (3, z2))
-    for step, zz in steps:
-        here(ym, zz, g, "gy", step, "g", "up")
-    accumulate(ym, False)
-    for step, zz in steps:
-        here(yp, zz, f, "gy", step, "f", "down")
-    accumulate(yp, False)
+    turn(o)
+    accumulate(y, o, True)
+    accumulate(ym, o, False)
+    accumulate(yp, o, False)
     for step, zz in steps:
         here(y2, zz, f, "gy", step, "f", "on")
         here(y2, zz, g, "gy", step, "g", "on")
-    accumulate(y2, False)
+    accumulate(y2, c, False)
+    accumulate(y2, o, False)
 
     def activate(m, carry):
         rows = pl.ds(pl.multiple_of(m * 64, 64), 64)
@@ -308,28 +320,37 @@
 
         lax.fori_loop(0, NY, tile, 0)
 
-    def first_y(step, zz):
+    def first_f(step, zz):
         send(T.at[y2, zz, f], R1.at[0, step], ("r1", step, "f"), up_y)
+
+    def first_g(step, zz):
         send(T.at[y2, zz, g], R1.at[1, step], ("r1", step, "g"), down_y)
 
-    def second_y(step, zz):
+    def plain_g(step, zz):
         send(T.at[yp, zz, g], R2.at[0, step, g], ("r2", step, "g", "up"), up_y)
+
+    def plain_f(step, zz):
         send(T.at[ym, zz, f], R2.at[1, step, f], ("r2", step, "f", "down"), down_y)
 
-    def third_y(step, zz):
+    def joined_f(step, zz):
         arrived(R1.at[0, step], "r1", step, "f")
         T[yp, zz, f] = (T[yp, zz, f].astype(F32) + R1[0, step].astype(F32)).astype(BF16)
         send(T.at[yp, zz, f], R2.at[0, step, f], ("r2", step, "f", "up"), up_y)
+
+    def joined_g(step, zz):
         arrived(R1.at[1, step], "r1", step, "g")
         T[ym, zz, g] = (T[ym, zz, g].astype(F32) + R1[1, step].astype(F32)).astype(BF16)
         send(T.at[ym, zz, g], R2.at[1, step, g], ("r2", step, "g", "down"), down_y)
 
     partials(y2)
-    first_y(0, z2)
+    first_f(0, z2)
+    first_g(0, z2)
     partials(yp)
     partials(ym)
-    second_y(0, z2)
-    first_y(1, zp)
+    plain_g(0, z2)
+    plain_f(0, z2)
+    first_f(1, zp)
+    first_g(2, zm)
 
     def write_sibling(n, yy, value):
         OS[n, yy] = value.astype(BF16).reshape(NE, CAP, YB)
@@ -337,10 +358,14 @@
     outputs(o, write_sibling)
     for n in range(2):
         send(OS.at[n], OR.at[n], ("part", n), sib)
-    third_y(0, z2)
-    first_y(2, zm)
-    second_y(1, zp)
-    second_y(2, zm)
+    joined_f(0, z2)
+    joined_g(0, z2)
+    first_f(2, zm)
+    first_g(1, zp)
+    plain_g(2, zm)
+    plain_f(1, zp)
+    plain_g(1, zp)
+    plain_f(2, zm)
 
     for n in range(2):
         arrived(OR.at[n], "part", n)
@@ -363,34 +388,43 @@
         copy.start()
         local.append(copy)
 
-    third_y(1, zp)
-    first_y(3, z)
-    third_y(2, zm)
-    second_y(3, z)
     partials(y)
-
-    def summed_y(step, zz):
+    joined_f(1, zp)
+    joined_g(2, zm)
+    joined_f(2, zm)
+    joined_g(1, zp)
+    first_f(3, z)
+    first_g(3, z)
+    plain_g(3, z)
+    plain_f(3, z)
+
+    def summed_y(step, zz, piece, kind):
         for d in range(2):
-            for piece, kind in ((f, "f"), (g, "g")):
-                arrived(R2.at[d, step, piece], "r2", step, kind, ("up", "down")[d])
-        return T[y, zz].astype(F32) + R2[0, step].astype(F32) + R2[1, step].astype(F32)
-
-    ZS[0] = summed_y(0, z2).astype(BF16)
+            arrived(R2.at[d, step, piece], "r2", step, kind, ("up", "down")[d])
+        return (
+            T[y, zz, piece].astype(F32)
+            + R2[0, step, piece].astype(F32)
+            + R2[1, step, piece].astype(F32)
+        )
+
+    ZS[0, f] = summed_y(0, z2, f, "f").astype(BF16)
     send(ZS.at[0, f], Z1.at[0], ("z1", "f"), up_z)
+    ZS[0, g] = summed_y(0, z2, g, "g").astype(BF16)
     send(ZS.at[0, g], Z1.at[1], ("z1", "g"), down_z)
-    third_y(3, z)
-
-    def second_z(n, zz, late, early, name, to):
-        FS[...] = summed_y(n, zz).reshape(2, 64, HC)
-        (piece, at), (first, first_at) = late, early
-        ZS[n, first] = FS[first_at].astype(BF16)
-        send(ZS.at[n, first], Z2.at[n - 1, first], ("z2", n, 0), to)
-        arrived(Z1.at[n - 1], "z1", name)
-        ZS[n, piece] = (FS[at] + Z1[n - 1].astype(F32)).astype(BF16)
-        send(ZS.at[n, piece], Z2.at[n - 1, piece], ("z2", n, 1), to)
-
-    second_z(1, zp, (f, c), (g, o), "f", up_z)
-    second_z(2, zm, (g, o), (f, c), "g", down_z)
+    total = summed_y(1, zp, f, "f")
+    arrived(Z1.at[0], "z1", "f")
+    ZS[1, f] = (total + Z1[0].astype(F32)).astype(BF16)
+    send(ZS.at[1, f], Z2.at[0, f], ("z2", "f", "up"), up_z)
+    total = summed_y(2, zm, g, "g")
+    arrived(Z1.at[1], "z1", "g")
+    ZS[2, g] = (total + Z1[1].astype(F32)).astype(BF16)
+    send(ZS.at[2, g], Z2.at[1, g], ("z2", "g", "down"), down_z)
+    ZS[2, f] = summed_y(2, zm, f, "f").astype(BF16)
+    send(ZS.at[2, f], Z2.at[1, f], ("z2", "f", "down"), down_z)
+    ZS[1, g] = summed_y(1, zp, g, "g").astype(BF16)
+    send(ZS.at[1, g], Z2.at[0, g], ("z2", "g", "up"), up_z)
+    joined_f(3, z)
+    joined_g(3, z)
 
     for n in range(2):
         local[n].wait()
@@ -399,25 +433,30 @@
                 for rows, _, fro, _ in partners(q)[crossing]:
                     which = 0 if rows is near else 1
                     arrived(BK.at[n, :, fro, rows], "back", n, crossing, q, which)
+    tn = (((0,), (0,)), ((), ()))
     for yy in range(NY):
         back = BK[0, yy].reshape(ROWS, YB)
-        out = sum(jnp.dot(SEL[n], back, preferred_element_type=F32) for n in (3, 2, 1))
+        out = sum(
+            lax.dot_general(SEL[n], back, tn, preferred_element_type=F32) for n in (3, 2, 1)
+        )
         back = BK[1, yy].reshape(ROWS, YB)
-        d_in = jnp.dot(SEL[0], back, preferred_element_type=F32)
+        d_in = lax.dot_general(SEL[0], back, tn, preferred_element_type=F32)
         for zz in range(NZ):
             cols = slice((zz * 4 + yy) * SH, (zz * 4 + yy + 1) * SH)
             lo_ref[:, cols] = out[:, zz * SH:(zz + 1) * SH].astype(BF16)
             dt_ref[:, cols] = d_in[:, zz * SH:(zz + 1) * SH].astype(BF16)
-    total = summed_y(3, z)
-    arrived(Z2.at[0, g], "z2", 1, 0)
-    arrived(Z2.at[0, f], "z2", 1, 1)
-    arrived(Z2.at[1, f], "z2", 2, 0)
-    arrived(Z2.at[1, g], "z2", 2, 1)
-    total = total + Z2[0].astype(F32) + Z2[1].astype(F32)
-    FS[...] = total.reshape(2, 64, HC)
-    send(FS.at[o], FR, ("fin",), sib)
+
+    def total_z(piece, kind):
+        total = summed_y(3, z, piece, kind)
+        arrived(Z2.at[0, piece], "z2", kind, "up")
+        arrived(Z2.at[1, piece], "z2", kind, "down")
+        return total + Z2[0, piece].astype(F32) + Z2[1, piece].astype(F32)
+
+    FS[...] = total_z(g, "g")
+    send(FS, FR, ("fin",), sib)
+    total = total_z(f, "f")
     for n, ref in enumerate((gg_ref, gu_ref, gd_ref)):
-        ref[0, :, half_c] = FS[c, :, n * HH:(n + 1) * HH]
+        ref[0, :, half_c] = total[:, n * HH:(n + 1) * HH]
     arrived(FR, "fin")
     for n, ref in enumerate((gg_ref, gu_ref, gd_ref)):
         ref[0, :, half_o] = FR[:, n * HH:(n + 1) * HH]
@@ -427,14 +466,28 @@
     assert len(numbers) <= N_SEM
 
 
+def hand_out(*refs):
+    count = len(refs) // 2
+    done = refs[-1]
+    copies = [
+        pltpu.make_async_copy(refs[n], refs[count + n], done.at[n]) for n in range(count)
+    ]
+    for copy in copies:
+        copy.start()
+    for copy in copies:
+        copy.wait()
+
+
 def shards(tokens, routes, gate_scale, w_gate, w_up, w_down, d_out):
     vm = pl.BlockSpec(memory_space=pltpu.VMEM)
+    hbm = pl.BlockSpec(memory_space=pltpu.HBM)
     grad = jax.ShapeDtypeStruct(w_gate.shape, F32)
     rows = jax.ShapeDtypeStruct(tokens.shape, BF16)
-    return pl.pallas_call(
+    results = (rows, rows, grad, grad, grad)
+    found = pl.pallas_call(
         kernel,
-        out_shape=(rows, rows, grad, grad, grad),
-        in_specs=[vm] * 7,
+        out_shape=results,
+        in_specs=[hbm] * 7,
         out_specs=(vm,) * 5,
         scratch_shapes=[
             pltpu.VMEM((NY, NZ, SH, HC), BF16),
@@ -444,7 +497,7 @@
             pltpu.VMEM((NY, YB, 2 * ROWS), BF16),
             pltpu.VMEM((NY, NE, CAP, YB), BF16),
             pltpu.VMEM((NY, NE, CAP, YB), BF16),
-            pltpu.VMEM((4, TOK, ROWS), BF16),
+            pltpu.VMEM((4, ROWS, TOK), BF16),
             pltpu.VMEM((2 * ROWS, HC), F32),
             pltpu.VMEM((2 * ROWS, HC), BF16),
             pltpu.VMEM((NY, NZ, SH, HC), BF16),
@@ -453,19 +506,34 @@
             pltpu.VMEM((2, 64, HC), BF16),
             pltpu.VMEM((2, SH, HC), BF16),
             pltpu.VMEM((3, SH, HC), BF16),
-            pltpu.VMEM((2, 64, HC), F32),
+            pltpu.VMEM((64, HC), F32),
             pltpu.VMEM((64, HC), F32),
             pltpu.VMEM((2, NY, NE, CAP, YB), BF16),
             pltpu.VMEM((2, NY, NE, CAP, YB), BF16),
             pltpu.VMEM((2, NY, NE, CAP, YB), BF16),
             pltpu.VMEM((2, NY, NE, CAP, YB), BF16),
+            pltpu.VMEM(tokens.shape, BF16),
+            pltpu.VMEM(tokens.shape, BF16),
+            pltpu.VMEM(routes.shape[::-1], jnp.int32),
+            pltpu.VMEM(routes.shape[::-1], F32),
             pltpu.SemaphoreType.DMA((N_SEM,)),
             pltpu.SemaphoreType.DMA((N_SEM,)),
         ],
         compiler_params=pltpu.CompilerParams(
-            collective_id=0, has_side_effects=True, vmem_limit_bytes=60 * 1024 * 1024
+            collective_id=0, has_side_effects=True, vmem_limit_bytes=VMEM_MB * 1024 * 1024
         ),
-    )(tokens, routes, gate_scale, w_gate, w_up, w_down, d_out)
+    )(*(
+        pltpu.with_memory_space_constraint(value, pltpu.HBM)
+        for value in (tokens, routes.T, gate_scale.T, w_gate, w_up, w_down, d_out)
+    ))
+    return pl.pallas_call(
+        hand_out,
+        out_shape=results,
+        in_specs=[vm] * 5,
+        out_specs=(hbm,) * 5,
+        scratch_shapes=[pltpu.SemaphoreType.DMA((5,))],
+        compiler_params=pltpu.CompilerParams(vmem_limit_bytes=8 * 1024 * 1024),
+    )(*found)
 
 
 def solution(mesh):

time: 119 us -> 108 us (0.908)
  local copies, waits for them, and re-layouts: 8.19 us -> 0 us
  Pallas kernels: 110 us -> 107 us
    unnamed x17 -> x0, local copies, waits for them, and re-layouts: 8.19 us -> none
    pallas_call x1 -> x2, Pallas kernels: 110 us -> 107 us  [the longest x1 105 us: shards(): pl.pallas_call(kernel, out_shape=results, in_specs=[hbm] * 7, out_specs=(...]
where the time goes in v3:
time: 108 us; the launch traced here: 107 us
  Pallas kernels  107 us (99%)
    pallas_call x1, Pallas kernels, shards(): pl.pallas_call(kernel, out_shape=results, in_specs=[hbm] * 7, out_specs=(...  105 us

profile of v3, /device:TPU:1, one launch (start us, length us, event | category | flops | bytes accessed | tf_op | source)
XLA Modules:
  0.0 107.2 jit_solution(1918128018362073495)
XLA Ops:
  0.6 105.2 %shard_map.110 = (bf16[192,2048]{1,0:T(8,128)(2,1)S(1)}, bf16[192,2048]{1,0:T(8,128)(2,1)S(1)}, f32[1,64,768]{2,1,0:T(8,128)S(1)}, f32[1,64,768]{2,1,0:T(8,128)S(1)}, f32[1,64,768]{2,1,0:T(8,128)S(1)}) custom-call(bf16[192,2048]{1,0:T(8,128)(2,1)} %tok_hbm.1, s32[6,192]{1,0:T(8,128)} %bitcast.2, f32[6,192]{1,0:T(8,128)} %bitcast.3, ...), custom_call_target="tpu_custom_call" | custom-call | tf_op jit(solution)/shard_map/pallas_call | solution.py:487
  105.8 1.4 %shard_map.111 = (bf16[192,2048]{1,0:T(8,128)(2,1)}, bf16[192,2048]{1,0:T(8,128)(2,1)}, f32[1,64,768]{2,1,0:T(8,128)}, f32[1,64,768]{2,1,0:T(8,128)}, f32[1,64,768]{2,1,0:T(8,128)}) custom-call(bf16[192,2048]{1,0:T(8,128)(2,1)S(1)} %get-tuple-element.10.refs_0_, bf16[192,2048]{1,0:T(8,128)(2,1)S(1)} %get-tuple-element.11.refs_1_, ...), custom_call_target="tpu_custom_call" | custom-call | tf_op jit(solution)/shard_map/pallas_call | solution.py:529

commit v4 on v3

--- a/solution.py
+++ b/solution.py
@@ -302,20 +302,15 @@
 
     nt = (((1,), (1,)), ((), ()))
 
-    def outputs(side, write):
+    def outputs(side, n, write):
         rows = pl.ds(pl.multiple_of(side * ROWS, ROWS), ROWS)
+        lo, hi = ((2 * HH, HC), (0, 2 * HH))[n]
 
         def tile(yy, carry):
-            out = lax.dot_general(
-                CAT[rows, 2 * HH:HC], W[yy, :, :, 2 * HH:HC].reshape(YB, HH), nt,
+            write(n, yy, lax.dot_general(
+                CAT[rows, lo:hi], W[yy, :, :, lo:hi].reshape(YB, hi - lo), nt,
                 preferred_element_type=F32,
-            )
-            write(0, yy, out)
-            d_in = lax.dot_general(
-                CAT[rows, 0:2 * HH], W[yy, :, :, 0:2 * HH].reshape(YB, 2 * HH), nt,
-                preferred_element_type=F32,
-            )
-            write(1, yy, d_in)
+            ))
             return carry
 
         lax.fori_loop(0, NY, tile, 0)
@@ -342,61 +337,63 @@
         T[ym, zz, g] = (T[ym, zz, g].astype(F32) + R1[1, step].astype(F32)).astype(BF16)
         send(T.at[ym, zz, g], R2.at[1, step, g], ("r2", step, "g", "down"), down_y)
 
-    partials(y2)
+    def partial(yy, zz):
+        rows = pl.ds(pl.multiple_of(zz * SH, SH), SH)
+        for ref, lo, hi in ((XT, 0, 256), (XT, 256, 512), (XT, 512, 768), (DT, 768, 1152)):
+            got = jnp.dot(ref[yy, rows], CAT[:, lo:hi], preferred_element_type=F32)
+            T[yy, zz, :, lo:hi] = got.astype(BF16)
+
+    partial(y2, z2)
     first_f(0, z2)
     first_g(0, z2)
     partials(yp)
+    plain_g(0, z2)
     partials(ym)
-    plain_g(0, z2)
     plain_f(0, z2)
-    first_f(1, zp)
-    first_g(2, zm)
+    partial(y2, zm)
+    partial(y2, zp)
+    partial(y2, z)
+    first_f(2, zm)
+    first_g(1, zp)
 
     def write_sibling(n, yy, value):
         OS[n, yy] = value.astype(BF16).reshape(NE, CAP, YB)
 
-    outputs(o, write_sibling)
     for n in range(2):
+        outputs(o, n, write_sibling)
         send(OS.at[n], OR.at[n], ("part", n), sib)
     joined_f(0, z2)
     joined_g(0, z2)
-    first_f(2, zm)
-    first_g(1, zp)
-    plain_g(2, zm)
-    plain_f(1, zp)
     plain_g(1, zp)
     plain_f(2, zm)
-
-    for n in range(2):
-        arrived(OR.at[n], "part", n)
 
     def write_own(n, yy, value):
         value = value + OR[n, yy].reshape(ROWS, YB).astype(F32)
         BS[n, yy] = value.astype(BF16).reshape(NE, CAP, YB)
 
-    outputs(c, write_own)
-    for crossing in (1, 0):
-        for n in range(2):
-            for q in range(4):
-                for rows, to, _, device in partners(q)[crossing]:
-                    which = 0 if rows is near else 1
-                    send(BS.at[n, :, to, rows], BK.at[n, :, j, rows],
-                         ("back", n, crossing, q, which), device)
+    def give_back(n, crossing):
+        for q in range(4):
+            for rows, to, _, device in partners(q)[crossing]:
+                which = 0 if rows is near else 1
+                send(BS.at[n, :, to, rows], BK.at[n, :, j, rows],
+                     ("back", n, crossing, q, which), device)
+
     local = []
     for n in range(2):
+        arrived(OR.at[n], "part", n)
+        outputs(c, n, write_own)
+        give_back(n, 1)
         copy = pltpu.make_async_copy(BS.at[n, :, j], BK.at[n, :, j], rs.at[number("stay", n)])
         copy.start()
         local.append(copy)
 
     partials(y)
-    joined_f(1, zp)
-    joined_g(2, zm)
     joined_f(2, zm)
     joined_g(1, zp)
-    first_f(3, z)
-    first_g(3, z)
-    plain_g(3, z)
-    plain_f(3, z)
+    first_f(1, zp)
+    first_g(2, zm)
+    plain_g(2, zm)
+    plain_f(1, zp)
 
     def summed_y(step, zz, piece, kind):
         for d in range(2):
@@ -411,6 +408,18 @@
     send(ZS.at[0, f], Z1.at[0], ("z1", "f"), up_z)
     ZS[0, g] = summed_y(0, z2, g, "g").astype(BF16)
     send(ZS.at[0, g], Z1.at[1], ("z1", "g"), down_z)
+    ZS[2, f] = summed_y(2, zm, f, "f").astype(BF16)
+    send(ZS.at[2, f], Z2.at[1, f], ("z2", "f", "down"), down_z)
+    ZS[1, g] = summed_y(1, zp, g, "g").astype(BF16)
+    send(ZS.at[1, g], Z2.at[0, g], ("z2", "g", "up"), up_z)
+    give_back(0, 0)
+    give_back(1, 0)
+    joined_f(1, zp)
+    joined_g(2, zm)
+    first_f(3, z)
+    first_g(3, z)
+    plain_g(3, z)
+    plain_f(3, z)
     total = summed_y(1, zp, f, "f")
     arrived(Z1.at[0], "z1", "f")
     ZS[1, f] = (total + Z1[0].astype(F32)).astype(BF16)
@@ -419,10 +428,6 @@
     arrived(Z1.at[1], "z1", "g")
     ZS[2, g] = (total + Z1[1].astype(F32)).astype(BF16)
     send(ZS.at[2, g], Z2.at[1, g], ("z2", "g", "down"), down_z)
-    ZS[2, f] = summed_y(2, zm, f, "f").astype(BF16)
-    send(ZS.at[2, f], Z2.at[1, f], ("z2", "f", "down"), down_z)
-    ZS[1, g] = summed_y(1, zp, g, "g").astype(BF16)
-    send(ZS.at[1, g], Z2.at[0, g], ("z2", "g", "up"), up_z)
     joined_f(3, z)
     joined_g(3, z)
 

time: 108 us -> 104 us (0.963)
  Pallas kernels: 107 us -> 103 us
    pallas_call x1, Pallas kernels: 105 us -> 102 us  [shards(): pl.pallas_call(kernel, out_shape=results, in_specs=[hbm] * 7, out_specs=(...]
where the time goes in v4:
time: 104 us
  Pallas kernels  103 us (99%)
    pallas_call x1, Pallas kernels, shards(): pl.pallas_call(kernel, out_shape=results, in_specs=[hbm] * 7, out_specs=(...  102 us

profile of v4, /device:TPU:1, one launch (start us, length us, event | category | flops | bytes accessed | tf_op | source)
XLA Modules:
  0.0 103.5 jit_solution(12939896684385506231)
XLA Ops:
  0.6 101.5 %shard_map.110 = (bf16[192,2048]{1,0:T(8,128)(2,1)S(1)}, bf16[192,2048]{1,0:T(8,128)(2,1)S(1)}, f32[1,64,768]{2,1,0:T(8,128)S(1)}, f32[1,64,768]{2,1,0:T(8,128)S(1)}, f32[1,64,768]{2,1,0:T(8,128)S(1)}) custom-call(bf16[192,2048]{1,0:T(8,128)(2,1)} %tok_hbm.1, s32[6,192]{1,0:T(8,128)} %bitcast.2, f32[6,192]{1,0:T(8,128)} %bitcast.3, ...), custom_call_target="tpu_custom_call" | custom-call | tf_op jit(solution)/shard_map/pallas_call | solution.py:492
  102.2 1.4 %shard_map.111 = (bf16[192,2048]{1,0:T(8,128)(2,1)}, bf16[192,2048]{1,0:T(8,128)(2,1)}, f32[1,64,768]{2,1,0:T(8,128)}, f32[1,64,768]{2,1,0:T(8,128)}, f32[1,64,768]{2,1,0:T(8,128)}) custom-call(bf16[192,2048]{1,0:T(8,128)(2,1)S(1)} %get-tuple-element.10.refs_0_, bf16[192,2048]{1,0:T(8,128)(2,1)S(1)} %get-tuple-element.11.refs_1_, ...), custom_call_target="tpu_custom_call" | custom-call | tf_op jit(solution)/shard_map/pallas_call | solution.py:534

commit v5 on v4

v5 whole, which is shorter than its diff:
```python
import jax
import jax.numpy as jnp
from jax import lax
from jax.experimental import pallas as pl
from jax.experimental.pallas import tpu as pltpu
from jax.sharding import PartitionSpec as P

CAP = 32
MESH = pl.DeviceIdType.MESH
F32 = jnp.float32
BF16 = jnp.bfloat16

NY, NZ, SH = 4, 4, 128
HH = 384
CW = (256, 128)
CO = (0, 256)
YB = NZ * SH
NE = 8
TOK = 192
ROWS = NE * CAP
N_SEM = 208
VMEM_MB = 50


def kernel(
    tok_hbm, rt_hbm, gs_hbm, wg_ref, wu_ref, wd_ref, do_hbm,
    lo_ref, dt_ref, gg_ref, gu_ref, gd_ref,
    W0, W1, WO0, WO1, X, D, XT, DT, SX, SD, SEL, A0, A1, C0, C1, T0, T1,
    RF0, RF1, RS0, RS1, ZF0, ZF1, Z20, Z21, ZS0, ZS1, FS0, FS1, FR0, FR1,
    OS, OR, BS, BK, tok_ref, do_ref, rt_ref, gs_ref, ss, rs,
):
    W, WO, ACC, CAT, T = (W0, W1), (WO0, WO1), (A0, A1), (C0, C1), (T0, T1)
    R1, R2, Z1, Z2, ZS = (RF0, RF1), (RS0, RS1), (ZF0, ZF1), (Z20, Z21), (ZS0, ZS1)
    FS, FR = (FS0, FS1), (FR0, FR1)
    i = lax.axis_index("dp")
    j = lax.axis_index("expert")
    c = lax.rem(i, 2)
    o = 1 - c
    p = lax.div(i, 2)
    y = lax.rem(p, 4)
    z = lax.div(p, 4)
    x = lax.div(j, 2)
    side = lax.rem(j, 2)
    yp, ym, y2 = lax.rem(y + 1, 4), lax.rem(y + 3, 4), lax.rem(y + 2, 4)
    zp, zm, z2 = lax.rem(z + 1, 4), lax.rem(z + 3, 4), lax.rem(z + 2, 4)
    zn = lax.rem(z + 3 + 2 * side, 4)

    def place(yy, zz, cc):
        return {"dp": (zz * 4 + yy) * 2 + cc}

    sib = place(y, z, o)
    up_y, down_y = place(yp, z, c), place(ym, z, c)
    up_z, down_z = place(y, zp, c), place(y, zm, c)

    near, far = pl.ds(0, 16), pl.ds(16, 16)

    def partners(q):
        to, fro = lax.rem(x + q, 4), lax.rem(x + 4 - q, 4)
        across = [
            (near, to * 2 + 1 - side, fro * 2 + 1 - side, {"expert": to * 2 + 1 - side}),
            (far, to * 2 + 1 - side, fro * 2 + 1 - side,
             {"dp": (zn * 4 + y) * 2 + c, "expert": to * 2 + 1 - side}),
        ]
        same = [(pl.ds(0, CAP), to * 2 + side, fro * 2 + side, {"expert": to * 2 + side})]
        return same if q else [], across

    numbers = {}

    def number(*name):
        return numbers.setdefault(name, len(numbers))

    sent = []

    def send(src, dst, name, to):
        k = number(*name)
        copy = pltpu.make_async_remote_copy(
            src_ref=src, dst_ref=dst, send_sem=ss.at[k], recv_sem=rs.at[k],
            device_id=to, device_id_type=MESH,
        )
        copy.start()
        sent.append(copy)

    def arrived(ref, *name):
        k = number(*name)
        pltpu.make_async_remote_copy(
            src_ref=ref, dst_ref=ref, send_sem=ss.at[k], recv_sem=rs.at[k],
            device_id=sib, device_id_type=MESH,
        ).wait_recv()

    def fetch(src, dst, *name):
        copy = pltpu.make_async_copy(src, dst, rs.at[number(*name)])
        copy.start()
        return copy

    f = pl.ds(pl.multiple_of(c * 64, 64), 64)
    g = pl.ds(pl.multiple_of(o * 64, 64), 64)

    def units(core, k):
        return pl.ds(pl.multiple_of(core * HH + CO[k], 128), CW[k])

    own, other = [[], []], [[], []]
    for k in range(2):
        for n, w_ref in enumerate((wg_ref, wu_ref, wd_ref)):
            cols = pl.ds(n * CW[k], CW[k])
            other[k].append(
                fetch(w_ref.at[0, :, units(o, k)], WO[k].at[:, cols], "other", k, n)
            )
            own[k].append(
                fetch(w_ref.at[0, :, units(c, k)], W[k].at[y, z, f, cols], "own", k, n)
            )
    loads = [
        fetch(rt_hbm, rt_ref, "load", "r"),
        fetch(gs_hbm, gs_ref, "load", "s"),
        fetch(tok_hbm, tok_ref, "load", "x"),
        fetch(do_hbm, do_ref, "load", "d"),
    ]
    barrier = pltpu.get_barrier_semaphore()
    greet = [sib, up_y, down_y, up_z, down_z]
    for q in range(4):
        same, across = partners(q)
        greet += [to for _, _, _, to in same + across]
    for to in greet:
        pl.semaphore_signal(barrier, inc=1, device_id=to, device_id_type=MESH)
    for k in range(2):
        for copy in other[k] + own[k]:
            copy.wait()
    pl.semaphore_wait(barrier, len(greet))

    def along(k, yy, zz, piece, name, to):
        send(W[k].at[yy, zz, piece], W[k].at[yy, zz, piece], (k,) + name, to)

    def here(k, yy, zz, piece, *name):
        arrived(W[k].at[yy, zz, piece], k, *name)

    def leave(k, kind, piece, way):
        to_z, to_y = (up_z, up_y) if way == "up" else (down_z, down_y)
        along(k, y, z, piece, ("gz", kind, way), to_z)
        along(k, y, z, piece, ("gy", 0, kind, way), to_y)

    for k in range(2):
        send(WO[k], W[k].at[y, z, f], ("sib", k), sib)
    leave(0, "f", f, "up")
    arrived(W[0].at[y, z, g], "sib", 0)
    leave(0, "g", g, "down")
    leave(0, "g", g, "up")
    leave(0, "f", f, "down")
    leave(1, "f", f, "up")
    arrived(W[1].at[y, z, g], "sib", 1)
    leave(1, "g", g, "down")
    leave(1, "g", g, "up")
    leave(1, "f", f, "down")

    shape = (ROWS, TOK)
    row = lax.broadcasted_iota(jnp.int32, shape, 0)
    row_e = lax.div(row, CAP)
    row_s = lax.rem(row, CAP).astype(F32)
    for copy in loads[:2]:
        copy.wait()
    scale = gs_ref[...]
    combine = scale / jnp.sum(scale, axis=0, keepdims=True)
    routes = rt_ref[...]
    named = jnp.zeros(shape, F32)
    weight = jnp.zeros(shape, F32)
    for s in range(6):
        same = routes[s:s + 1, :] == row_e
        named = jnp.where(same, 1.0, named)
        weight = jnp.where(same, combine[s:s + 1, :], weight)
    earlier = (
        lax.broadcasted_iota(jnp.int32, (TOK, TOK), 0)
        < lax.broadcasted_iota(jnp.int32, (TOK, TOK), 1)
    ).astype(F32).astype(BF16)
    position = jnp.dot(named.astype(BF16), earlier, preferred_element_type=F32)
    chosen = jnp.where(position == row_s, named, 0.0)
    weight = weight * chosen
    slot_weight = jnp.sum(weight, axis=1, keepdims=True)
    select = chosen.astype(BF16)
    SEL[0] = select
    rest = weight
    for n in range(1, 4):
        part = rest.astype(BF16)
        SEL[n] = part
        rest = rest - part.astype(F32)

    def columns(ref, yy):
        return jnp.concatenate(
            [ref[:, (zz * 4 + yy) * SH:(zz * 4 + yy + 1) * SH] for zz in range(NZ)], axis=1
        )

    for copy in loads[2:]:
        copy.wait()
    for yy in range(NY):
        rows = jnp.dot(select, columns(tok_ref, yy), preferred_element_type=F32)
        SX[yy] = rows.astype(BF16).reshape(NE, CAP, YB)
        rows = jnp.dot(select, columns(do_ref, yy), preferred_element_type=F32)
        SD[yy] = (rows * slot_weight).astype(BF16).reshape(NE, CAP, YB)

    mine = c * NE + j
    rows_out = ((SX, X, "x"), (SD, D, "d"))

    def exchange(crossing):
        for src, dst, what in rows_out:
            for q in range(4):
                for rows, to, _, device in partners(q)[crossing]:
                    which = 0 if rows is near else 1
                    send(src.at[:, to, rows], dst.at[:, mine, rows],
                         ("to", what, crossing, q, which), device)

    exchange(0)
    local = [fetch(src.at[:, j], dst.at[:, mine], "keep", what) for src, dst, what in rows_out]

    def spread_y(k, step, zz, piece, kind):
        along(k, y, zz, piece, ("gy", step, kind, "up"), up_y)
        along(k, y, zz, piece, ("gy", step, kind, "down"), down_y)

    def onward_f(k, step, zz):
        here(k, ym, zz, f, "gy", step, "f", "up")
        along(k, ym, zz, f, ("gy", step, "f", "on"), up_y)

    def onward_g(k, step, zz):
        here(k, yp, zz, g, "gy", step, "g", "down")
        along(k, yp, zz, g, ("gy", step, "g", "on"), down_y)

    def onward_z(k):
        here(k, y, zm, f, "gz", "f", "up")
        along(k, y, zm, f, ("gz", "f", "on"), up_z)
        here(k, y, zp, g, "gz", "g", "down")
        along(k, y, zp, g, ("gz", "g", "on"), down_z)

    onward_f(0, 0, z)
    onward_g(0, 0, z)
    onward_z(0)
    spread_y(0, 1, zm, f, "f")
    spread_y(0, 2, zp, g, "g")
    exchange(1)
    onward_f(1, 0, z)
    onward_g(1, 0, z)
    here(0, y, zm, g, "gz", "g", "up")
    spread_y(0, 1, zm, g, "g")
    here(0, y, zp, f, "gz", "f", "down")
    spread_y(0, 2, zp, f, "f")
    onward_z(1)
    onward_f(0, 1, zm)
    onward_g(0, 2, zp)
    here(0, y, z2, f, "gz", "f", "on")
    spread_y(0, 3, z2, f, "f")
    here(0, y, z2, g, "gz", "g", "on")
    spread_y(0, 3, z2, g, "g")
    here(1, y, zm, g, "gz", "g", "up")
    here(1, y, zp, f, "gz", "f", "down")
    for step, zz in ((1, zm), (2, zp)):
        spread_y(1, step, zz, f, "f")
        spread_y(1, step, zz, g, "g")
    onward_g(0, 1, zm)
    onward_f(0, 2, zp)
    onward_f(0, 3, z2)
    onward_g(0, 3, z2)
    for step, zz in ((1, zm), (2, zp)):
        onward_f(1, step, zz)
        onward_g(1, step, zz)
    for n, (_, dst, what) in enumerate(rows_out):
        local[n].wait()
        for q in range(4):
            for crossing in range(2):
                for rows, _, fro, _ in partners(q)[crossing]:
                    which = 0 if rows is near else 1
                    arrived(dst.at[:, c * NE + fro, rows], "to", what, crossing, q, which)
        block = dst.at[:, pl.ds(c * NE, NE)]
        send(block, block, ("rows", what), sib)

    def turn(m):
        def body(yy, carry):
            cols = pl.ds(pl.multiple_of(m * ROWS, ROWS), ROWS)
            blocks = pl.ds(m * NE, NE)
            XT[yy, :, cols] = X[yy, blocks].reshape(ROWS, YB).T
            DT[yy, :, cols] = D[yy, blocks].reshape(ROWS, YB).T
            return carry

        lax.fori_loop(0, NY, body, 0)

    tiles = (
        ((0, 0, 256), (0, 256, 512), (1, 512, 768)),
        ((0, 0, 256), (1, 256, 384)),
    )

    def accumulate(k, yy, m, first=False):
        rows = pl.ds(pl.multiple_of(m * ROWS, ROWS), ROWS)
        blocks = pl.ds(m * NE, NE)
        for which, lo, hi in tiles[k]:
            got = jnp.dot(
                (X, D)[which][yy, blocks].reshape(ROWS, YB),
                W[k][yy, :, :, lo:hi].reshape(YB, hi - lo),
                preferred_element_type=F32,
            )
            if first:
                ACC[k][rows, lo:hi] = got
            else:
                ACC[k][rows, lo:hi] += got

    steps = ((0, z), (1, zm), (2, zp), (3, z2))

    def wait_m(k):
        for step, zz in steps:
            here(k, ym, zz, g, "gy", step, "g", "up")

    def wait_p(k):
        for step, zz in steps:
            here(k, yp, zz, f, "gy", step, "f", "down")

    def wait_2(k):
        for step, zz in steps:
            here(k, y2, zz, f, "gy", step, "f", "on")
            here(k, y2, zz, g, "gy", step, "g", "on")

    turn(c)
    accumulate(0, y, c, True)
    wait_m(0)
    accumulate(0, ym, c)
    wait_p(0)
    accumulate(0, yp, c)
    wait_2(0)
    accumulate(0, y2, c)
    here(1, y, z2, f, "gz", "f", "on")
    spread_y(1, 3, z2, f, "f")
    here(1, y, z2, g, "gz", "g", "on")
    spread_y(1, 3, z2, g, "g")
    arrived(X.at[:, pl.ds(o * NE, NE)], "rows", "x")
    arrived(D.at[:, pl.ds(o * NE, NE)], "rows", "d")
    turn(o)
    accumulate(0, y, o, True)
    accumulate(0, ym, o)
    accumulate(0, yp, o)
    accumulate(0, y2, o)

    def activate(k):
        w = CW[k]

        def body(m, carry):
            rows = pl.ds(pl.multiple_of(m * 64, 64), 64)
            gate, up, d_hidden = (ACC[k][rows, n * w:(n + 1) * w] for n in range(3))
            sig = jax.nn.sigmoid(gate)
            act = gate * sig
            CAT[k][rows, 0:w] = (
                d_hidden * up * sig * (1.0 + gate * (1.0 - sig))
            ).astype(BF16)
            CAT[k][rows, w:2 * w] = (d_hidden * act).astype(BF16)
            CAT[k][rows, 2 * w:3 * w] = (act * up).astype(BF16)
            return carry

        lax.fori_loop(0, 2 * ROWS // 64, body, 0)

    def partials(k, yy):
        for which, lo, hi in tiles[k]:
            got = jnp.dot(
                (XT, DT)[which][yy], CAT[k][:, lo:hi], preferred_element_type=F32
            )
            T[k][yy, :, :, lo:hi] = got.astype(BF16).reshape(NZ, SH, hi - lo)

    def partial(k, yy, zz):
        rows = pl.ds(pl.multiple_of(zz * SH, SH), SH)
        for which, lo, hi in tiles[k]:
            got = jnp.dot(
                (XT, DT)[which][yy, rows], CAT[k][:, lo:hi], preferred_element_type=F32
            )
            T[k][yy, zz, :, lo:hi] = got.astype(BF16)

    nt = (((1,), (1,)), ((), ()))

    def outputs(side_, n, write):
        rows = pl.ds(pl.multiple_of(side_ * ROWS, ROWS), ROWS)

        def tile(yy, carry):
            total = None
            for k in range(2):
                lo, hi = ((2 * CW[k], 3 * CW[k]), (0, 2 * CW[k]))[n]
                got = lax.dot_general(
                    CAT[k][rows, lo:hi], W[k][yy, :, :, lo:hi].reshape(YB, hi - lo), nt,
                    preferred_element_type=F32,
                )
                total = got if total is None else total + got
            write(n, yy, total)
            return carry

        lax.fori_loop(0, NY, tile, 0)

    def first_f(k, step, zz):
        send(T[k].at[y2, zz, f], R1[k].at[0, step], ("r1", k, step, "f"), up_y)

    def first_g(k, step, zz):
        send(T[k].at[y2, zz, g], R1[k].at[1, step], ("r1", k, step, "g"), down_y)

    def plain_g(k, step, zz):
        send(T[k].at[yp, zz, g], R2[k].at[0, step, g], ("r2", k, step, "g", "up"), up_y)

    def plain_f(k, step, zz):
        send(T[k].at[ym, zz, f], R2[k].at[1, step, f], ("r2", k, step, "f", "down"), down_y)

    def joined_f(k, step, zz):
        arrived(R1[k].at[0, step], "r1", k, step, "f")
        T[k][yp, zz, f] = (
            T[k][yp, zz, f].astype(F32) + R1[k][0, step].astype(F32)
        ).astype(BF16)
        send(T[k].at[yp, zz, f], R2[k].at[0, step, f], ("r2", k, step, "f", "up"), up_y)

    def joined_g(k, step, zz):
        arrived(R1[k].at[1, step], "r1", k, step, "g")
        T[k][ym, zz, g] = (
            T[k][ym, zz, g].astype(F32) + R1[k][1, step].astype(F32)
        ).astype(BF16)
        send(T[k].at[ym, zz, g], R2[k].at[1, step, g], ("r2", k, step, "g", "down"), down_y)

    def summed_y(k, step, zz, piece, kind):
        for d in range(2):
            arrived(R2[k].at[d, step, piece], "r2", k, step, kind, ("up", "down")[d])
        return (
            T[k][y, zz, piece].astype(F32)
            + R2[k][0, step, piece].astype(F32)
            + R2[k][1, step, piece].astype(F32)
        )

    def far_z(k):
        ZS[k][0, f] = summed_y(k, 0, z2, f, "f").astype(BF16)
        send(ZS[k].at[0, f], Z1[k].at[0], ("z1", k, "f"), up_z)
        ZS[k][0, g] = summed_y(k, 0, z2, g, "g").astype(BF16)
        send(ZS[k].at[0, g], Z1[k].at[1], ("z1", k, "g"), down_z)

    def plain_z(k):
        ZS[k][2, f] = summed_y(k, 2, zm, f, "f").astype(BF16)
        send(ZS[k].at[2, f], Z2[k].at[1, f], ("z2", k, "f", "down"), down_z)
        ZS[k][1, g] = summed_y(k, 1, zp, g, "g").astype(BF16)
        send(ZS[k].at[1, g], Z2[k].at[0, g], ("z2", k, "g", "up"), up_z)

    def joined_z(k):
        total = summed_y(k, 1, zp, f, "f")
        arrived(Z1[k].at[0], "z1", k, "f")
        ZS[k][1, f] = (total + Z1[k][0].astype(F32)).astype(BF16)
        send(ZS[k].at[1, f], Z2[k].at[0, f], ("z2", k, "f", "up"), up_z)
        total = summed_y(k, 2, zm, g, "g")
        arrived(Z1[k].at[1], "z1", k, "g")
        ZS[k][2, g] = (total + Z1[k][1].astype(F32)).astype(BF16)
        send(ZS[k].at[2, g], Z2[k].at[1, g], ("z2", k, "g", "down"), down_z)

    def total_z(k, piece, kind):
        total = summed_y(k, 3, z, piece, kind)
        arrived(Z2[k].at[0, piece], "z2", k, kind, "up")
        arrived(Z2[k].at[1, piece], "z2", k, kind, "down")
        return total + Z2[k][0, piece].astype(F32) + Z2[k][1, piece].astype(F32)

    grads = (gg_ref, gu_ref, gd_ref)

    def finish(k):
        w = CW[k]
        FS[k][...] = total_z(k, g, "g")
        send(FS[k], FR[k], ("fin", k), sib)
        total = total_z(k, f, "f")
        for n, ref in enumerate(grads):
            ref[0, :, units(c, k)] = total[:, n * w:(n + 1) * w]

    def close(k):
        w = CW[k]
        arrived(FR[k], "fin", k)
        for n, ref in enumerate(grads):
            ref[0, :, units(o, k)] = FR[k][:, n * w:(n + 1) * w]

    activate(0)
    onward_f(1, 3, z2)
    onward_g(1, 3, z2)
    partial(0, y2, z2)
    first_f(0, 0, z2)
    first_g(0, 0, z2)
    partials(0, yp)
    plain_g(0, 0, z2)
    partials(0, ym)
    plain_f(0, 0, z2)
    partial(0, y2, zm)
    partial(0, y2, zp)
    partial(0, y2, z)
    first_f(0, 2, zm)
    first_g(0, 1, zp)
    for m, first in ((c, True), (o, True)):
        accumulate(1, y, m, first)
    wait_m(1)
    wait_p(1)
    for m in (c, o):
        accumulate(1, ym, m)
        accumulate(1, yp, m)
    wait_2(1)
    for m in (c, o):
        accumulate(1, y2, m)
    activate(1)
    for yy in (y2, yp, ym):
        partial(1, yy, z2)
    first_f(1, 0, z2)
    first_g(1, 0, z2)
    plain_g(1, 0, z2)
    plain_f(1, 0, z2)

    def write_sibling(n, yy, value):
        OS[n, yy] = value.astype(BF16).reshape(NE, CAP, YB)

    outputs(o, 0, write_sibling)
    send(OS.at[0], OR.at[0], ("part", 0), sib)
    joined_f(0, 0, z2)
    joined_g(0, 0, z2)
    plain_g(0, 1, zp)
    plain_f(0, 2, zm)
    outputs(o, 1, write_sibling)
    send(OS.at[1], OR.at[1], ("part", 1), sib)

    def write_own(n, yy, value):
        value = value + OR[n, yy].reshape(ROWS, YB).astype(F32)
        BS[n, yy] = value.astype(BF16).reshape(NE, CAP, YB)

    def give_back(n, crossing):
        for q in range(4):
            for rows, to, _, device in partners(q)[crossing]:
                which = 0 if rows is near else 1
                send(BS.at[n, :, to, rows], BK.at[n, :, j, rows],
                     ("back", n, crossing, q, which), device)

    local = []
    for n in range(2):
        arrived(OR.at[n], "part", n)
        outputs(c, n, write_own)
        if n == 0:
            give_back(0, 1)
        local.append(fetch(BS.at[n, :, j], BK.at[n, :, j], "stay", n))

    joined_f(1, 0, z2)
    joined_g(1, 0, z2)
    joined_f(0, 2, zm)
    joined_g(0, 1, zp)
    first_f(0, 1, zp)
    first_g(0, 2, zm)
    plain_g(0, 2, zm)
    plain_f(0, 1, zp)
    partials(0, y)
    far_z(0)
    give_back(0, 0)
    for yy in (y2, yp, ym):
        for zz in (zm, zp, z):
            partial(1, yy, zz)
    partials(1, y)
    far_z(1)
    plain_z(0)
    give_back(1, 1)
    joined_f(0, 1, zp)
    joined_g(0, 2, zm)
    first_f(0, 3, z)
    first_g(0, 3, z)
    first_f(1, 2, zm)
    first_g(1, 1, zp)
    first_f(1, 1, zp)
    first_g(1, 2, zm)
    plain_g(0, 3, z)
    plain_f(0, 3, z)
    plain_g(1, 1, zp)
    plain_f(1, 2, zm)
    joined_z(0)
    give_back(1, 0)
    joined_f(1, 2, zm)
    joined_g(1, 1, zp)
    first_f(1, 3, z)
    first_g(1, 3, z)
    plain_g(1, 2, zm)
    plain_f(1, 1, zp)
    joined_f(1, 1, zp)
    joined_g(1, 2, zm)
    joined_f(0, 3, z)
    joined_g(0, 3, z)
    plain_g(1, 3, z)
    plain_f(1, 3, z)
    plain_z(1)
    joined_f(1, 3, z)
    joined_g(1, 3, z)
    joined_z(1)

    for n in range(2):
        local[n].wait()
        for q in range(4):
            for crossing in range(2):
                for rows, _, fro, _ in partners(q)[crossing]:
                    which = 0 if rows is near else 1
                    arrived(BK.at[n, :, fro, rows], "back", n, crossing, q, which)
    tn = (((0,), (0,)), ((), ()))
    for yy in range(NY):
        back = BK[0, yy].reshape(ROWS, YB)
        out = sum(
            lax.dot_general(SEL[n], back, tn, preferred_element_type=F32) for n in (3, 2, 1)
        )
        back = BK[1, yy].reshape(ROWS, YB)
        d_in = lax.dot_general(SEL[0], back, tn, preferred_element_type=F32)
        for zz in range(NZ):
            cols = slice((zz * 4 + yy) * SH, (zz * 4 + yy + 1) * SH)
            lo_ref[:, cols] = out[:, zz * SH:(zz + 1) * SH].astype(BF16)
            dt_ref[:, cols] = d_in[:, zz * SH:(zz + 1) * SH].astype(BF16)

    finish(0)
    finish(1)
    close(0)
    close(1)

    for copy in sent:
        copy.wait_send()
    assert len(numbers) <= N_SEM


def hand_out(*refs):
    count = len(refs) // 2
    done = refs[-1]
    copies = [
        pltpu.make_async_copy(refs[n], refs[count + n], done.at[n]) for n in range(count)
    ]
    for copy in copies:
        copy.start()
    for copy in copies:
        copy.wait()


def shards(tokens, routes, gate_scale, w_gate, w_up, w_down, d_out):
    vm = pl.BlockSpec(memory_space=pltpu.VMEM)
    hbm = pl.BlockSpec(memory_space=pltpu.HBM)
    grad = jax.ShapeDtypeStruct(w_gate.shape, F32)
    rows = jax.ShapeDtypeStruct(tokens.shape, BF16)
    results = (rows, rows, grad, grad, grad)

    def chunks(kind, *lead):
        return [pltpu.VMEM((*lead, 3 * w), kind) for w in CW]

    found = pl.pallas_call(
        kernel,
        out_shape=results,
        in_specs=[hbm] * 7,
        out_specs=(vm,) * 5,
        scratch_shapes=[
            *chunks(BF16, NY, NZ, SH),
            *chunks(BF16, 64),
            pltpu.VMEM((NY, 2 * NE, CAP, YB), BF16),
            pltpu.VMEM((NY, 2 * NE, CAP, YB), BF16),
            pltpu.VMEM((NY, YB, 2 * ROWS), BF16),
            pltpu.VMEM((NY, YB, 2 * ROWS), BF16),
            pltpu.VMEM((NY, NE, CAP, YB), BF16),
            pltpu.VMEM((NY, NE, CAP, YB), BF16),
            pltpu.VMEM((4, ROWS, TOK), BF16),
            *chunks(F32, 2 * ROWS),
            *chunks(BF16, 2 * ROWS),
            *chunks(BF16, NY, NZ, SH),
            *chunks(BF16, 2, NZ, 64),
            *chunks(BF16, 2, NZ, SH),
            *chunks(BF16, 2, 64),
            *chunks(BF16, 2, SH),
            *chunks(BF16, 3, SH),
            *chunks(F32, 64),
            *chunks(F32, 64),
            pltpu.VMEM((2, NY, NE, CAP, YB), BF16),
            pltpu.VMEM((2, NY, NE, CAP, YB), BF16),
            pltpu.VMEM((2, NY, NE, CAP, YB), BF16),
            pltpu.VMEM((2, NY, NE, CAP, YB), BF16),
            pltpu.VMEM(tokens.shape, BF16),
            pltpu.VMEM(tokens.shape, BF16),
            pltpu.VMEM(routes.shape[::-1], jnp.int32),
            pltpu.VMEM(routes.shape[::-1], F32),
            pltpu.SemaphoreType.DMA((N_SEM,)),
            pltpu.SemaphoreType.DMA((N_SEM,)),
        ],
        compiler_params=pltpu.CompilerParams(
            collective_id=0, has_side_effects=True, vmem_limit_bytes=VMEM_MB * 1024 * 1024
        ),
    )(*(
        pltpu.with_memory_space_constraint(value, pltpu.HBM)
        for value in (tokens, routes.T, gate_scale.T, w_gate, w_up, w_down, d_out)
    ))
    return pl.pallas_call(
        hand_out,
        out_shape=results,
        in_specs=[vm] * 5,
        out_specs=(hbm,) * 5,
        scratch_shapes=[pltpu.SemaphoreType.DMA((5,))],
        compiler_params=pltpu.CompilerParams(vmem_limit_bytes=8 * 1024 * 1024),
    )(*found)


def solution(mesh):
    tok = P(("dp", "expert"), None)
    wei = P("expert", "dp", None)
    return jax.shard_map(
        shards,
        mesh=mesh,
        in_specs=(tok, tok, tok, wei, wei, wei, tok),
        out_specs=(tok, tok, wei, wei, wei),
        check_vma=False,
    )
```

time: 104 us -> 102 us (0.981)
  Pallas kernels: 103 us -> 101 us
    pallas_call x1, Pallas kernels: 102 us -> 100 us  [shards(): pl.pallas_call(kernel, out_shape=results, in_specs=[hbm] * 7, out_specs=(...]
where the time goes in v5:
time: 102 us
  Pallas kernels  101 us (99%)
    pallas_call x1, Pallas kernels, shards(): pl.pallas_call(kernel, out_shape=results, in_specs=[hbm] * 7, out_specs=(...  100 us

profile of v5, /device:TPU:1, one launch (start us, length us, event | category | flops | bytes accessed | tf_op | source)
XLA Modules:
  0.0 102.1 jit_solution(9560181206197169837)
XLA Ops:
  0.6 100.0 %shard_map.110 = (bf16[192,2048]{1,0:T(8,128)(2,1)S(1)}, bf16[192,2048]{1,0:T(8,128)(2,1)S(1)}, f32[1,64,768]{2,1,0:T(8,128)S(1)}, f32[1,64,768]{2,1,0:T(8,128)S(1)}, f32[1,64,768]{2,1,0:T(8,128)S(1)}) custom-call(bf16[192,2048]{1,0:T(8,128)(2,1)} %tok_hbm.1, s32[6,192]{1,0:T(8,128)} %bitcast.2, f32[6,192]{1,0:T(8,128)} %bitcast.3, ...), custom_call_target="tpu_custom_call" | custom-call | tf_op jit(solution)/shard_map/pallas_call | solution.py:629
  100.7 1.4 %shard_map.111 = (bf16[192,2048]{1,0:T(8,128)(2,1)}, bf16[192,2048]{1,0:T(8,128)(2,1)}, f32[1,64,768]{2,1,0:T(8,128)}, f32[1,64,768]{2,1,0:T(8,128)}, f32[1,64,768]{2,1,0:T(8,128)}) custom-call(bf16[192,2048]{1,0:T(8,128)(2,1)S(1)} %get-tuple-element.10.refs_0_, bf16[192,2048]{1,0:T(8,128)(2,1)S(1)} %get-tuple-element.11.refs_1_, ...), custom_call_target="tpu_custom_call" | custom-call | tf_op jit(solution)/shard_map/pallas_call | solution.py:672

commit v6 on v5

--- a/solution.py
+++ b/solution.py
@@ -18,7 +18,7 @@
 NE = 8
 TOK = 192
 ROWS = NE * CAP
-N_SEM = 208
+N_SEM = 240
 VMEM_MB = 50
 
 
@@ -267,15 +267,16 @@
         block = dst.at[:, pl.ds(c * NE, NE)]
         send(block, block, ("rows", what), sib)
 
-    def turn(m):
-        def body(yy, carry):
+    def turn(m, first, last):
+        def body(step, carry):
+            yy = lax.rem(y2 + step, NY)
             cols = pl.ds(pl.multiple_of(m * ROWS, ROWS), ROWS)
             blocks = pl.ds(m * NE, NE)
             XT[yy, :, cols] = X[yy, blocks].reshape(ROWS, YB).T
             DT[yy, :, cols] = D[yy, blocks].reshape(ROWS, YB).T
             return carry
 
-        lax.fori_loop(0, NY, body, 0)
+        lax.fori_loop(first, last, body, 0)
 
     tiles = (
         ((0, 0, 256), (0, 256, 512), (1, 512, 768)),
@@ -311,7 +312,11 @@
             here(k, y2, zz, f, "gy", step, "f", "on")
             here(k, y2, zz, g, "gy", step, "g", "on")
 
-    turn(c)
+    turn(c, 0, NY)
+    here(1, y, z2, f, "gz", "f", "on")
+    spread_y(1, 3, z2, f, "f")
+    here(1, y, z2, g, "gz", "g", "on")
+    spread_y(1, 3, z2, g, "g")
     accumulate(0, y, c, True)
     wait_m(0)
     accumulate(0, ym, c)
@@ -319,13 +324,9 @@
     accumulate(0, yp, c)
     wait_2(0)
     accumulate(0, y2, c)
-    here(1, y, z2, f, "gz", "f", "on")
-    spread_y(1, 3, z2, f, "f")
-    here(1, y, z2, g, "gz", "g", "on")
-    spread_y(1, 3, z2, g, "g")
     arrived(X.at[:, pl.ds(o * NE, NE)], "rows", "x")
     arrived(D.at[:, pl.ds(o * NE, NE)], "rows", "d")
-    turn(o)
+    turn(o, 0, 1)
     accumulate(0, y, o, True)
     accumulate(0, ym, o)
     accumulate(0, yp, o)
@@ -365,22 +366,36 @@
 
     nt = (((1,), (1,)), ((), ()))
 
-    def outputs(side_, n, write):
+    def output(side_, n, yy):
         rows = pl.ds(pl.multiple_of(side_ * ROWS, ROWS), ROWS)
-
-        def tile(yy, carry):
-            total = None
-            for k in range(2):
-                lo, hi = ((2 * CW[k], 3 * CW[k]), (0, 2 * CW[k]))[n]
-                got = lax.dot_general(
-                    CAT[k][rows, lo:hi], W[k][yy, :, :, lo:hi].reshape(YB, hi - lo), nt,
-                    preferred_element_type=F32,
-                )
-                total = got if total is None else total + got
-            write(n, yy, total)
-            return carry
-
-        lax.fori_loop(0, NY, tile, 0)
+        total = None
+        for k in range(2):
+            lo, hi = ((2 * CW[k], 3 * CW[k]), (0, 2 * CW[k]))[n]
+            got = lax.dot_general(
+                CAT[k][rows, lo:hi], W[k][yy, :, :, lo:hi].reshape(YB, hi - lo), nt,
+                preferred_element_type=F32,
+            )
+            total = got if total is None else total + got
+        return total
+
+    def output_sibling(n):
+        for yy in range(NY):
+            OS[n, yy] = output(o, n, yy).astype(BF16).reshape(NE, CAP, YB)
+            send(OS.at[n, yy], OR.at[n, yy], ("part", n, yy), sib)
+
+    def output_own(n):
+        for yy in range(NY):
+            value = output(c, n, yy)
+            arrived(OR.at[n, yy], "part", n, yy)
+            value = value + OR[n, yy].reshape(ROWS, YB).astype(F32)
+            BS[n, yy] = value.astype(BF16).reshape(NE, CAP, YB)
+
+    def give_back(n, crossing):
+        for q in range(4):
+            for rows, to, _, device in partners(q)[crossing]:
+                which = 0 if rows is near else 1
+                send(BS.at[n, :, to, rows], BK.at[n, :, j, rows],
+                     ("back", n, crossing, q, which), device)
 
     def first_f(k, step, zz):
         send(T[k].at[y2, zz, f], R1[k].at[0, step], ("r1", k, step, "f"), up_y)
@@ -467,14 +482,14 @@
     partial(0, y2, z2)
     first_f(0, 0, z2)
     first_g(0, 0, z2)
-    partials(0, yp)
+    turn(o, 1, NY)
+    partial(0, yp, z2)
     plain_g(0, 0, z2)
-    partials(0, ym)
+    partial(0, ym, z2)
     plain_f(0, 0, z2)
     partial(0, y2, zm)
+    first_f(0, 2, zm)
     partial(0, y2, zp)
-    partial(0, y2, z)
-    first_f(0, 2, zm)
     first_g(0, 1, zp)
     for m, first in ((c, True), (o, True)):
         accumulate(1, y, m, first)
@@ -487,60 +502,46 @@
     for m in (c, o):
         accumulate(1, y2, m)
     activate(1)
+    output_sibling(0)
+    joined_f(0, 0, z2)
+    joined_g(0, 0, z2)
+    partial(0, yp, zp)
+    plain_g(0, 1, zp)
+    partial(0, ym, zm)
+    plain_f(0, 2, zm)
+    output_own(0)
+    give_back(0, 1)
+    local = [fetch(BS.at[0, :, j], BK.at[0, :, j], "stay", 0)]
     for yy in (y2, yp, ym):
         partial(1, yy, z2)
     first_f(1, 0, z2)
     first_g(1, 0, z2)
     plain_g(1, 0, z2)
     plain_f(1, 0, z2)
-
-    def write_sibling(n, yy, value):
-        OS[n, yy] = value.astype(BF16).reshape(NE, CAP, YB)
-
-    outputs(o, 0, write_sibling)
-    send(OS.at[0], OR.at[0], ("part", 0), sib)
-    joined_f(0, 0, z2)
-    joined_g(0, 0, z2)
-    plain_g(0, 1, zp)
-    plain_f(0, 2, zm)
-    outputs(o, 1, write_sibling)
-    send(OS.at[1], OR.at[1], ("part", 1), sib)
-
-    def write_own(n, yy, value):
-        value = value + OR[n, yy].reshape(ROWS, YB).astype(F32)
-        BS[n, yy] = value.astype(BF16).reshape(NE, CAP, YB)
-
-    def give_back(n, crossing):
-        for q in range(4):
-            for rows, to, _, device in partners(q)[crossing]:
-                which = 0 if rows is near else 1
-                send(BS.at[n, :, to, rows], BK.at[n, :, j, rows],
-                     ("back", n, crossing, q, which), device)
-
-    local = []
-    for n in range(2):
-        arrived(OR.at[n], "part", n)
-        outputs(c, n, write_own)
-        if n == 0:
-            give_back(0, 1)
-        local.append(fetch(BS.at[n, :, j], BK.at[n, :, j], "stay", n))
-
-    joined_f(1, 0, z2)
-    joined_g(1, 0, z2)
+    partial(0, yp, zm)
+    partial(0, ym, zp)
     joined_f(0, 2, zm)
     joined_g(0, 1, zp)
     first_f(0, 1, zp)
     first_g(0, 2, zm)
     plain_g(0, 2, zm)
     plain_f(0, 1, zp)
-    partials(0, y)
+    output_sibling(1)
+    partial(0, y, z2)
     far_z(0)
+    output_own(1)
+    local.append(fetch(BS.at[1, :, j], BK.at[1, :, j], "stay", 1))
+    joined_f(1, 0, z2)
+    joined_g(1, 0, z2)
+    for zz in (zm, zp, z):
+        partial(0, y, zz)
+    for yy in (y2, yp, ym):
+        partial(0, yy, z)
     give_back(0, 0)
     for yy in (y2, yp, ym):
         for zz in (zm, zp, z):
             partial(1, yy, zz)
     partials(1, y)
-    far_z(1)
     plain_z(0)
     give_back(1, 1)
     joined_f(0, 1, zp)
@@ -555,6 +556,7 @@
     plain_f(0, 3, z)
     plain_g(1, 1, zp)
     plain_f(1, 2, zm)
+    far_z(1)
     joined_z(0)
     give_back(1, 0)
     joined_f(1, 2, zm)

time: 102 us -> 99.4 us (0.975)
  Pallas kernels: 101 us -> 98.5 us
    pallas_call x1, Pallas kernels: 100 us -> 97.2 us  [shards(): pl.pallas_call(kernel, out_shape=results, in_specs=[hbm] * 7, out_specs=(...]
where the time goes in v6:
time: 99.4 us; the launch traced here: 99.3 us
  Pallas kernels  98.5 us (99%)
    pallas_call x1, Pallas kernels, shards(): pl.pallas_call(kernel, out_shape=results, in_specs=[hbm] * 7, out_specs=(...  97.2 us

profile of v6, /device:TPU:1, one launch (start us, length us, event | category | flops | bytes accessed | tf_op | source)
XLA Modules:
  0.0 99.3 jit_solution(7496372558078680835)
XLA Ops:
  0.6 97.2 %shard_map.110 = (bf16[192,2048]{1,0:T(8,128)(2,1)S(1)}, bf16[192,2048]{1,0:T(8,128)(2,1)S(1)}, f32[1,64,768]{2,1,0:T(8,128)S(1)}, f32[1,64,768]{2,1,0:T(8,128)S(1)}, f32[1,64,768]{2,1,0:T(8,128)S(1)}) custom-call(bf16[192,2048]{1,0:T(8,128)(2,1)} %tok_hbm.1, s32[6,192]{1,0:T(8,128)} %bitcast.2, f32[6,192]{1,0:T(8,128)} %bitcast.3, ...), custom_call_target="tpu_custom_call" | custom-call | tf_op jit(solution)/shard_map/pallas_call | solution.py:631
  97.8 1.4 %shard_map.111 = (bf16[192,2048]{1,0:T(8,128)(2,1)}, bf16[192,2048]{1,0:T(8,128)(2,1)}, f32[1,64,768]{2,1,0:T(8,128)}, f32[1,64,768]{2,1,0:T(8,128)}, f32[1,64,768]{2,1,0:T(8,128)}) custom-call(bf16[192,2048]{1,0:T(8,128)(2,1)S(1)} %get-tuple-element.10.refs_0_, bf16[192,2048]{1,0:T(8,128)(2,1)S(1)} %get-tuple-element.11.refs_1_, ...), custom_call_target="tpu_custom_call" | custom-call | tf_op jit(solution)/shard_map/pallas_call | solution.py:674

commit v7 on v6

--- a/solution.py
+++ b/solution.py
@@ -252,20 +252,27 @@
         spread_y(1, step, zz, g, "g")
     onward_g(0, 1, zm)
     onward_f(0, 2, zp)
+    def fro(q, crossing):
+        return lax.rem(x + 4 - q, 4) * 2 + (1 - side if crossing else side)
+
+    def pass_on(crossing):
+        for n, (_, dst, what) in enumerate(rows_out):
+            for q in range(4):
+                if q == 0 and not crossing:
+                    local[n].wait()
+                for rows, _, block, _ in partners(q)[crossing]:
+                    which = 0 if rows is near else 1
+                    arrived(dst.at[:, c * NE + block, rows], "to", what, crossing, q, which)
+                ready = dst.at[:, c * NE + fro(q, crossing)]
+                send(ready, ready, ("rows", what, crossing, q), sib)
+
+    pass_on(0)
     onward_f(0, 3, z2)
     onward_g(0, 3, z2)
     for step, zz in ((1, zm), (2, zp)):
         onward_f(1, step, zz)
         onward_g(1, step, zz)
-    for n, (_, dst, what) in enumerate(rows_out):
-        local[n].wait()
-        for q in range(4):
-            for crossing in range(2):
-                for rows, _, fro, _ in partners(q)[crossing]:
-                    which = 0 if rows is near else 1
-                    arrived(dst.at[:, c * NE + fro, rows], "to", what, crossing, q, which)
-        block = dst.at[:, pl.ds(c * NE, NE)]
-        send(block, block, ("rows", what), sib)
+    pass_on(1)
 
     def turn(m, first, last):
         def body(step, carry):
@@ -312,24 +319,26 @@
             here(k, y2, zz, f, "gy", step, "f", "on")
             here(k, y2, zz, g, "gy", step, "g", "on")
 
-    turn(c, 0, NY)
-    here(1, y, z2, f, "gz", "f", "on")
-    spread_y(1, 3, z2, f, "f")
-    here(1, y, z2, g, "gz", "g", "on")
-    spread_y(1, 3, z2, g, "g")
+    turn(c, 0, 1)
     accumulate(0, y, c, True)
     wait_m(0)
     accumulate(0, ym, c)
     wait_p(0)
     accumulate(0, yp, c)
-    wait_2(0)
-    accumulate(0, y2, c)
-    arrived(X.at[:, pl.ds(o * NE, NE)], "rows", "x")
-    arrived(D.at[:, pl.ds(o * NE, NE)], "rows", "d")
+    here(1, y, z2, f, "gz", "f", "on")
+    spread_y(1, 3, z2, f, "f")
+    here(1, y, z2, g, "gz", "g", "on")
+    spread_y(1, 3, z2, g, "g")
+    for _, dst, what in rows_out:
+        for crossing in range(2):
+            for q in range(4):
+                arrived(dst.at[:, o * NE + fro(q, crossing)], "rows", what, crossing, q)
     turn(o, 0, 1)
     accumulate(0, y, o, True)
     accumulate(0, ym, o)
     accumulate(0, yp, o)
+    wait_2(0)
+    accumulate(0, y2, c)
     accumulate(0, y2, o)
 
     def activate(k):
@@ -482,6 +491,7 @@
     partial(0, y2, z2)
     first_f(0, 0, z2)
     first_g(0, 0, z2)
+    turn(c, 1, NY)
     turn(o, 1, NY)
     partial(0, yp, z2)
     plain_g(0, 0, z2)
@@ -546,14 +556,12 @@
     give_back(1, 1)
     joined_f(0, 1, zp)
     joined_g(0, 2, zm)
-    first_f(0, 3, z)
-    first_g(0, 3, z)
     first_f(1, 2, zm)
     first_g(1, 1, zp)
     first_f(1, 1, zp)
     first_g(1, 2, zm)
-    plain_g(0, 3, z)
-    plain_f(0, 3, z)
+    first_f(0, 3, z)
+    first_g(0, 3, z)
     plain_g(1, 1, zp)
     plain_f(1, 2, zm)
     far_z(1)
@@ -561,20 +569,22 @@
     give_back(1, 0)
     joined_f(1, 2, zm)
     joined_g(1, 1, zp)
-    first_f(1, 3, z)
-    first_g(1, 3, z)
     plain_g(1, 2, zm)
     plain_f(1, 1, zp)
     joined_f(1, 1, zp)
     joined_g(1, 2, zm)
+    first_f(1, 3, z)
+    first_g(1, 3, z)
+    plain_g(0, 3, z)
+    plain_f(0, 3, z)
     joined_f(0, 3, z)
     joined_g(0, 3, z)
     plain_g(1, 3, z)
     plain_f(1, 3, z)
     plain_z(1)
+    joined_z(1)
     joined_f(1, 3, z)
     joined_g(1, 3, z)
-    joined_z(1)
 
     for n in range(2):
         local[n].wait()

time: 99.4 us -> 100 us (level)
  no operation moved by 1% of the time
where the time goes in v7:
time: 100 us
  Pallas kernels  99.3 us (99%)
    pallas_call x1, Pallas kernels, shards(): pl.pallas_call(kernel, out_shape=results, in_specs=[hbm] * 7, out_specs=(...  98 us

profile of v7, /device:TPU:1, one launch (start us, length us, event | category | flops | bytes accessed | tf_op | source)
XLA Modules:
  0.0 100.1 jit_solution(7430920405886038368)
XLA Ops:
  0.6 98.0 %shard_map.110 = (bf16[192,2048]{1,0:T(8,128)(2,1)S(1)}, bf16[192,2048]{1,0:T(8,128)(2,1)S(1)}, f32[1,64,768]{2,1,0:T(8,128)S(1)}, f32[1,64,768]{2,1,0:T(8,128)S(1)}, f32[1,64,768]{2,1,0:T(8,128)S(1)}) custom-call(bf16[192,2048]{1,0:T(8,128)(2,1)} %tok_hbm.1, s32[6,192]{1,0:T(8,128)} %bitcast.2, f32[6,192]{1,0:T(8,128)} %bitcast.3, ...), custom_call_target="tpu_custom_call" | custom-call | tf_op jit(solution)/shard_map/pallas_call | solution.py:641
  98.6 1.4 %shard_map.111 = (bf16[192,2048]{1,0:T(8,128)(2,1)}, bf16[192,2048]{1,0:T(8,128)(2,1)}, f32[1,64,768]{2,1,0:T(8,128)}, f32[1,64,768]{2,1,0:T(8,128)}, f32[1,64,768]{2,1,0:T(8,128)}) custom-call(bf16[192,2048]{1,0:T(8,128)(2,1)S(1)} %get-tuple-element.10.refs_0_, bf16[192,2048]{1,0:T(8,128)(2,1)S(1)} %get-tuple-element.11.refs_1_, ...), custom_call_target="tpu_custom_call" | custom-call | tf_op jit(solution)/shard_map/pallas_call | solution.py:684

commit v8 on v6

--- a/solution.py
+++ b/solution.py
@@ -546,14 +546,12 @@
     give_back(1, 1)
     joined_f(0, 1, zp)
     joined_g(0, 2, zm)
-    first_f(0, 3, z)
-    first_g(0, 3, z)
     first_f(1, 2, zm)
     first_g(1, 1, zp)
     first_f(1, 1, zp)
     first_g(1, 2, zm)
-    plain_g(0, 3, z)
-    plain_f(0, 3, z)
+    first_f(0, 3, z)
+    first_g(0, 3, z)
     plain_g(1, 1, zp)
     plain_f(1, 2, zm)
     far_z(1)
@@ -561,20 +559,22 @@
     give_back(1, 0)
     joined_f(1, 2, zm)
     joined_g(1, 1, zp)
-    first_f(1, 3, z)
-    first_g(1, 3, z)
     plain_g(1, 2, zm)
     plain_f(1, 1, zp)
     joined_f(1, 1, zp)
     joined_g(1, 2, zm)
+    plain_g(0, 3, z)
+    plain_f(0, 3, z)
+    first_f(1, 3, z)
+    first_g(1, 3, z)
     joined_f(0, 3, z)
     joined_g(0, 3, z)
     plain_g(1, 3, z)
     plain_f(1, 3, z)
     plain_z(1)
+    joined_z(1)
     joined_f(1, 3, z)
     joined_g(1, 3, z)
-    joined_z(1)
 
     for n in range(2):
         local[n].wait()

time: 99.4 us -> 99.4 us (level)
  no operation moved by 1% of the time
where the time goes in v8:
time: 99.4 us; the launch traced here: 99.3 us
  Pallas kernels  98.5 us (99%)
    pallas_call x1, Pallas kernels, shards(): pl.pallas_call(kernel, out_shape=results, in_specs=[hbm] * 7, out_specs=(...  97.2 us

profile of v8, /device:TPU:1, one launch (start us, length us, event | category | flops | bytes accessed | tf_op | source)
XLA Modules:
  0.0 99.3 jit_solution(16594091720054167450)
XLA Ops:
  0.6 97.2 %shard_map.110 = (bf16[192,2048]{1,0:T(8,128)(2,1)S(1)}, bf16[192,2048]{1,0:T(8,128)(2,1)S(1)}, f32[1,64,768]{2,1,0:T(8,128)S(1)}, f32[1,64,768]{2,1,0:T(8,128)S(1)}, f32[1,64,768]{2,1,0:T(8,128)S(1)}) custom-call(bf16[192,2048]{1,0:T(8,128)(2,1)} %tok_hbm.1, s32[6,192]{1,0:T(8,128)} %bitcast.2, f32[6,192]{1,0:T(8,128)} %bitcast.3, ...), custom_call_target="tpu_custom_call" | custom-call | tf_op jit(solution)/shard_map/pallas_call | solution.py:631
  97.8 1.4 %shard_map.111 = (bf16[192,2048]{1,0:T(8,128)(2,1)}, bf16[192,2048]{1,0:T(8,128)(2,1)}, f32[1,64,768]{2,1,0:T(8,128)}, f32[1,64,768]{2,1,0:T(8,128)}, f32[1,64,768]{2,1,0:T(8,128)}) custom-call(bf16[192,2048]{1,0:T(8,128)(2,1)S(1)} %get-tuple-element.10.refs_0_, bf16[192,2048]{1,0:T(8,128)(2,1)S(1)} %get-tuple-element.11.refs_1_, ...), custom_call_target="tpu_custom_call" | custom-call | tf_op jit(solution)/shard_map/pallas_call | solution.py:674

commit v9 on v8

--- a/solution.py
+++ b/solution.py
@@ -563,10 +563,10 @@
     plain_f(1, 1, zp)
     joined_f(1, 1, zp)
     joined_g(1, 2, zm)
+    first_f(1, 3, z)
+    first_g(1, 3, z)
     plain_g(0, 3, z)
     plain_f(0, 3, z)
-    first_f(1, 3, z)
-    first_g(1, 3, z)
     joined_f(0, 3, z)
     joined_g(0, 3, z)
     plain_g(1, 3, z)

time: 99.4 us -> 99.4 us (level)
  no operation moved by 1% of the time
where the time goes in v9:
time: 99.4 us; the launch traced here: 99.3 us
  Pallas kernels  98.5 us (99%)
    pallas_call x1, Pallas kernels, shards(): pl.pallas_call(kernel, out_shape=results, in_specs=[hbm] * 7, out_specs=(...  97.2 us

profile of v9, /device:TPU:1, one launch (start us, length us, event | category | flops | bytes accessed | tf_op | source)
XLA Modules:
  0.0 99.3 jit_solution(9248744690713211459)
XLA Ops:
  0.6 97.2 %shard_map.110 = (bf16[192,2048]{1,0:T(8,128)(2,1)S(1)}, bf16[192,2048]{1,0:T(8,128)(2,1)S(1)}, f32[1,64,768]{2,1,0:T(8,128)S(1)}, f32[1,64,768]{2,1,0:T(8,128)S(1)}, f32[1,64,768]{2,1,0:T(8,128)S(1)}) custom-call(bf16[192,2048]{1,0:T(8,128)(2,1)} %tok_hbm.1, s32[6,192]{1,0:T(8,128)} %bitcast.2, f32[6,192]{1,0:T(8,128)} %bitcast.3, ...), custom_call_target="tpu_custom_call" | custom-call | tf_op jit(solution)/shard_map/pallas_call | solution.py:631
  97.8 1.4 %shard_map.111 = (bf16[192,2048]{1,0:T(8,128)(2,1)}, bf16[192,2048]{1,0:T(8,128)(2,1)}, f32[1,64,768]{2,1,0:T(8,128)}, f32[1,64,768]{2,1,0:T(8,128)}, f32[1,64,768]{2,1,0:T(8,128)}) custom-call(bf16[192,2048]{1,0:T(8,128)(2,1)S(1)} %get-tuple-element.10.refs_0_, bf16[192,2048]{1,0:T(8,128)(2,1)S(1)} %get-tuple-element.11.refs_1_, ...), custom_call_target="tpu_custom_call" | custom-call | tf_op jit(solution)/shard_map/pallas_call | solution.py:674

commit v10 on v9

--- a/solution.py
+++ b/solution.py
@@ -542,8 +542,8 @@
         for zz in (zm, zp, z):
             partial(1, yy, zz)
     partials(1, y)
+    give_back(1, 1)
     plain_z(0)
-    give_back(1, 1)
     joined_f(0, 1, zp)
     joined_g(0, 2, zm)
     first_f(1, 2, zm)

time: 99.4 us -> 99.4 us (level)
  no operation moved by 1% of the time
where the time goes in v10:
time: 99.4 us; the launch traced here: 99.3 us
  Pallas kernels  98.5 us (99%)
    pallas_call x1, Pallas kernels, shards(): pl.pallas_call(kernel, out_shape=results, in_specs=[hbm] * 7, out_specs=(...  97.2 us

profile of v10, /device:TPU:1, one launch (start us, length us, event | category | flops | bytes accessed | tf_op | source)
XLA Modules:
  0.0 99.3 jit_solution(3769549477891146311)
XLA Ops:
  0.6 97.2 %shard_map.110 = (bf16[192,2048]{1,0:T(8,128)(2,1)S(1)}, bf16[192,2048]{1,0:T(8,128)(2,1)S(1)}, f32[1,64,768]{2,1,0:T(8,128)S(1)}, f32[1,64,768]{2,1,0:T(8,128)S(1)}, f32[1,64,768]{2,1,0:T(8,128)S(1)}) custom-call(bf16[192,2048]{1,0:T(8,128)(2,1)} %tok_hbm.1, s32[6,192]{1,0:T(8,128)} %bitcast.2, f32[6,192]{1,0:T(8,128)} %bitcast.3, ...), custom_call_target="tpu_custom_call" | custom-call | tf_op jit(solution)/shard_map/pallas_call | solution.py:631
  97.8 1.4 %shard_map.111 = (bf16[192,2048]{1,0:T(8,128)(2,1)}, bf16[192,2048]{1,0:T(8,128)(2,1)}, f32[1,64,768]{2,1,0:T(8,128)}, f32[1,64,768]{2,1,0:T(8,128)}, f32[1,64,768]{2,1,0:T(8,128)}) custom-call(bf16[192,2048]{1,0:T(8,128)(2,1)S(1)} %get-tuple-element.10.refs_0_, bf16[192,2048]{1,0:T(8,128)(2,1)S(1)} %get-tuple-element.11.refs_1_, ...), custom_call_target="tpu_custom_call" | custom-call | tf_op jit(solution)/shard_map/pallas_call | solution.py:674
